TPU v7x, 256 devices: a whole 4x4x8 slice. The times are simulated.
256 devices in a mesh: inp: 32 (over x, z_lo, core), frq: 8 (over y, z_hi).
Axes of the slice: x: 4, y: 4, z: 8 (z_hi: 2, z_lo: 4; z = z_hi * 4 + z_lo), core: 2. Of those that a mesh axis runs over, the one named last changes fastest.
Arguments:
- voltages: bfloat16 [1024, 32, 2048], P('inp', 'frq'), may hold values from -6 to 6
- history: bfloat16 [1024, 3, 2048], P('inp'), may hold values from -6 to 6
- window: float32 [4, 2048], replicated, may hold values from -3 to 3
Outputs:
- visibilities: float32 [1024, 32, 2, 1024], P('frq', 'inp')
All inputs are finite; a program needn't handle non-finite values.
Results may differ from a plain program's by a relative error of at most 0.0003.
Values may be sent and summed in bfloat16 or wider, within the bound.
No kernel may reach another device: no remote copies, remote signals or barrier semaphores. Data moves between devices by JAX's collectives and lax.ppermute only.
A program may use at most 64 MiB of HBM per device.

v0:
```python
import math

import jax
import jax.numpy as jnp
from jax import lax
from jax.sharding import PartitionSpec as P

SAMPLES = 2048
CH_DEV = 1


def shifted(block, axis, distance):
    devices = range(lax.axis_size(axis))
    route = [(i - distance, i) for i in devices if i - distance in devices]
    return lax.ppermute(block, axis, route)


def copy_for_each(x, axis):
    devices = lax.axis_size(axis)
    return lax.all_to_all(jnp.broadcast_to(x[None], (devices, *x.shape)), axis, 0, 0, tiled=True)


def in_order(parts, dim):
    dims = list(parts.shape[1:])
    dims[dim] *= parts.shape[0]
    return jnp.moveaxis(parts, 0, dim).reshape(dims)


def gathered_copies(x, axis, dim):
    parts = copy_for_each(x, axis)
    return in_order(parts, dim)


def dft_table(channels, samples, first_bin):
    chan_bins = jnp.arange(channels, dtype=jnp.int32) + first_bin
    positions = jnp.arange(samples, dtype=jnp.int32)
    turns = chan_bins[:, None] * positions[None, :] % samples
    phases = turns.astype(jnp.float32) * (2.0 * math.pi / samples)
    scaling = 1.0 / math.sqrt(samples)
    return jnp.stack([jnp.cos(phases), -jnp.sin(phases)], axis=1) * scaling


def gram_rows(samples_in, first_row, row_count):
    chans = samples_in.shape[0]
    frames = samples_in.shape[1]
    inputs = samples_in.shape[3]
    left_rows = lax.dynamic_slice_in_dim(samples_in, first_row, row_count, 3)
    real_left = left_rows.reshape(chans, 2 * frames, row_count)
    imag_left = jnp.stack([left_rows[:, :, 1], -left_rows[:, :, 0]], axis=2).reshape(
        chans, 2 * frames, row_count
    )
    stacked = jnp.stack([real_left, imag_left], axis=1)
    all_cols = samples_in.reshape(chans, 2 * frames, inputs)
    return jnp.einsum("cjkr,cks->rcjs", stacked, all_cols, precision=lax.Precision.HIGHEST)


def body(voltages, history, window):
    taps_back = window.shape[0] - 1
    frames = voltages.shape[1]
    earlier = shifted(voltages[:, frames - taps_back :, :], "frq", 1)
    leading = jnp.where(lax.axis_index("frq") == 0, history, earlier)
    extended = jnp.concatenate([leading, voltages], axis=1).astype(jnp.float32)
    filtered = window[0] * extended[:, 0:frames, :]
    for tap_index in range(1, taps_back + 1):
        filtered = filtered + window[tap_index] * extended[:, tap_index : tap_index + frames, :]
    channels = CH_DEV * lax.axis_size("inp")
    first_bin = (SAMPLES // 2 - channels) // 2
    weights = dft_table(channels, SAMPLES, first_bin)
    spectra = jnp.einsum("cpn,itn->ctpi", weights, filtered, precision=lax.Precision.HIGHEST)
    turned = lax.all_to_all(spectra, "inp", split_axis=0, concat_axis=3, tiled=True)
    total_frames = frames * lax.axis_size("frq")
    tile_rows = turned.shape[3] // lax.axis_size("frq")
    anchor = lax.axis_index("frq") * tile_rows
    summed = gram_rows(gathered_copies(turned, "frq", 1), anchor, tile_rows)
    return summed / total_frames


def solution(mesh):
    return jax.shard_map(
        body,
        mesh=mesh,
        in_specs=(P("inp", "frq", None), P("inp", None, None), P()),
        out_specs=P("frq", "inp", None, None),
        check_vma=False,
    )
```

profile of v0, /device:TPU:33, one launch (start us, length us, event | category | flops | bytes accessed | tf_op | source)
XLA Modules:
  0.0 72.8 jit_solution(4308384924391291497)
XLA Ops:
  0.0 0.0 copy-start
  0.0 0.0 copy-start.2
  0.0 0.0 copy-start.1
  0.0 1.4 %slice.34 = bf16[32,3,2048]{2,1,0:T(4,128)(2,1)S(1)} slice(bf16[32,4,2048]{2,1,0:T(4,128)(2,1)} %param.3), slice={[0:32], [1:4], [0:2048]} | slice | bytes 786432 | tf_op jit(solution)/shard_map/slice | solution.py:60
  1.5 0.3 copy.22
  1.8 7.9 %collective-permute-start = (bf16[32,3,2048]{2,0,1:T(8,128)(2,1)S(1)}, bf16[32,3,2048]{2,0,1:T(8,128)(2,1)S(1)}, u32[]{:S(2)}, u32[]{:S(2)}) collective-permute-start(bf16[32,3,2048]{2,0,1:T(8,128)(2,1)S(1)} %copy.22), channel_id=1, source_target_pairs={{0,1},{1,2},{2,3},{3,4},{4,5},{5,6},{6,7},{8,9},{9,10},{10,11},{11... | collective-permute-start | bytes 1179656 | tf_op jit(solution)/shard_map/ppermute | solution.py:15
  9.7 1.1 %fusion.17 = (f32[32,1,2048]{2,0,1:T(8,128)S(1)}, f32[32,1,2048]{2,0,1:T(8,128)S(1)}) fusion(s32[32]{0:T(128)S(1)} %iota_add_fusion), kind=kLoop, calls=%fused_computation.29 | loop fusion | flops 983040 | bytes 524416 | tf_op jit(solution)/shard_map/cos | solution.py:40
  10.8 0.0 copy-done.2
  10.9 11.0 %collective-permute-done = bf16[32,3,2048]{2,0,1:T(8,128)(2,1)S(1)} collective-permute-done((bf16[32,3,2048]{2,0,1:T(8,128)(2,1)S(1)}, bf16[32,3,2048]{2,0,1:T(8,128)(2,1)S(1)}, u32[]{:S(2)}, u32[]{:S(2)}) %collective-permute-start) | collective-permute-done | bytes 393248 | tf_op jit(solution)/shard_map/ppermute | solution.py:15
  21.9 0.0 copy-done.1
  22.0 0.3 copy.14
  22.3 0.0 copy-done
  22.3 0.5 maximum_convert_fusion
  22.8 0.9 %fusion.2 = f32[32,4,2048,1]{2,1,0,3:T(4,128)S(1)} fusion(f32[32,7,2048]{2,1,0:T(8,128)S(1)} %maximum_convert_fusion, f32[2048]{0:T(1024)S(1)} %bitcast.34, f32[2048]{0:T(1024)S(1)} %bitcast.35, f32[2048]{0:T(1024)S(1)} %bitcast.33, f32[2048]{0:T(1024)S(1)} %bitcast.32), kind=kLoop, calls=%fused_computation.5 | loop fusion | flops 1835008 | bytes 5275648 | tf_op jit(solution)/shard_map/add | solution.py:65
  23.7 1.8 %convolution_bitcast_fusion = f32[32,4,2,32]{0,3,2,1:T(8,128)S(1)} fusion(f32[32,4,2048,1]{2,1,0,3:T(4,128)S(1)} %fusion.2, f32[32,1,2048]{2,0,1:T(8,128)S(1)} %get-tuple-element.12, f32[32,1,2048]{2,0,1:T(8,128)S(1)} %get-tuple-element.11), kind=kOutput, calls=%fused_computation.2 | convolution fusion | flops 201588736 | bytes 1605632 | tf_op jit(solution)/shard_map/cpn,itn->ctpi/dot_general | solution.py:69
  25.5 0.1 copy.16
  25.6 0.2 reshape.127
  25.8 17.6 %all_to_all.20 = f32[32,1,256]{2,1,0:T(1,128)S(1)} all-to-all(f32[32,1,256]{2,1,0:T(1,128)S(1)} %reshape.127), channel_id=1, replica_groups=mesh['inp'=32,'frq'=8] {'inp'}, dimensions={0} | all-to-all | bytes 65536 | tf_op jit(solution)/shard_map/all_to_all | solution.py:70
  43.3 0.5 broadcast.119
  43.8 0.7 reduce
  44.6 0.1 reshape.128
  44.8 0.1 broadcast_in_dim.4
  44.9 0.8 %broadcast_in_dim.5 = f32[8,1,4,2,1024]{4,3,2,1,0:T(2,128)} broadcast(f32[4,2,1024]{2,1,0:T(2,128)S(1)} %broadcast_in_dim.4), dimensions={2,3,4} | broadcast | bytes 294912 | tf_op jit(solution)/shard_map/broadcast_in_dim | solution.py:20
  45.7 10.1 %all-to-all-start.1 = ((f32[8,1,4,2,1024]{4,3,2,1,0:T(2,128)}), f32[8,1,4,2,1024]{4,3,2,1,0:T(2,128)S(1)}, u32[]{:S(2)}, u32[]{:S(2)}) async-start(f32[8,1,4,2,1024]{4,3,2,1,0:T(2,128)} %broadcast_in_dim.5), calls=%async_computation.1 | async-start | bytes 524288 | tf_op jit(solution)/shard_map/all_to_all | solution.py:20
  55.8 14.3 %all-to-all-done.1 = f32[8,1,4,2,1024]{4,3,2,1,0:T(2,128)S(1)} async-done(((f32[8,1,4,2,1024]{4,3,2,1,0:T(2,128)}), f32[8,1,4,2,1024]{4,3,2,1,0:T(2,128)S(1)}, u32[]{:S(2)}, u32[]{:S(2)}) %all-to-all-start.1) | async-done | bytes 262176 | tf_op jit(solution)/shard_map/all_to_all | solution.py:20
  70.1 0.1 constant_dynamic-slice_fusion
  70.3 0.2 reshape.125
  70.5 1.0 %fusion = f32[128,1,2,1024]{0,3,2,1:T(8,128)S(1)} fusion(f32[64,1024,1]{1,0,2:T(8,128)S(1)} %reshape.125, f32[1,1,64,128]{3,2,1,0:T(8,128)S(1)} %bitcast.31, f32[1,1,64,128]{3,2,1,0:T(8,128)S(1)} %bitcast.30), kind=kOutput, calls=%fused_computation.1 | convolution fusion | flops 201605120 | bytes 1376256 | tf_op jit(solution)/shard_map/cjkr,cks->rcjs/dot_general | solution.py:54
  71.5 1.3 %copy.18 = f32[128,1,2,1024]{3,2,1,0:T(2,128)} copy(f32[128,1,2,1024]{0,3,2,1:T(8,128)S(1)} %fusion) | data formatting | bytes 2097152 | tf_op jit(solution)/shard_map/div | solution.py:75
  (6 shorter events, 0.1 us)
Async XLA Ops:
  0.0 22.3 %copy-start = (bf16[32,4,2048]{2,1,0:T(4,128)(2,1)S(1)}, bf16[32,4,2048]{2,1,0:T(4,128)(2,1)}, u32[]{:S(2)}) copy-start(bf16[32,4,2048]{2,1,0:T(4,128)(2,1)} %param.3) | copy-start | bytes 1572868
  0.0 10.8 %copy-start.2 = (f32[4,2048]{1,0:T(4,128)S(1)}, f32[4,2048]{1,0:T(4,128)}, u32[]{:S(2)}) copy-start(f32[4,2048]{1,0:T(4,128)} %param.5) | copy-start | bytes 98308
  0.0 21.9 %copy-start.1 = (bf16[32,3,2048]{2,0,1:T(8,128)(2,1)S(1)}, bf16[32,3,2048]{2,0,1:T(8,128)(2,1)}, u32[]{:S(2)}) copy-start(bf16[32,3,2048]{2,0,1:T(8,128)(2,1)} %param.4) | copy-start | bytes 1179652
  1.8 20.1 %collective-permute-start = (bf16[32,3,2048]{2,0,1:T(8,128)(2,1)S(1)}, bf16[32,3,2048]{2,0,1:T(8,128)(2,1)S(1)}, u32[]{:S(2)}, u32[]{:S(2)}) collective-permute-start(bf16[32,3,2048]{2,0,1:T(8,128)(2,1)S(1)} %copy.22), channel_id=1, source_target_pairs={{0,1},{1,2},{2,3},{3,4},{4,5},{5,6},{6,7},{8,9},{9,10},{10,11},{11... | collective-permute-start | bytes 1179656 | tf_op jit(solution)/shard_map/ppermute | solution.py:15
  45.7 24.4 %all-to-all-start.1 = ((f32[8,1,4,2,1024]{4,3,2,1,0:T(2,128)}), f32[8,1,4,2,1024]{4,3,2,1,0:T(2,128)S(1)}, u32[]{:S(2)}, u32[]{:S(2)}) async-start(f32[8,1,4,2,1024]{4,3,2,1,0:T(2,128)} %broadcast_in_dim.5), calls=%async_computation.1 | async-start | bytes 524288 | tf_op jit(solution)/shard_map/all_to_all | solution.py:20
where the time goes:
time: 73.1 us; the launch traced here: 72.8 us
  waiting for transfers between devices  25.4 us (35%)
  starting transfers between devices  18 us (25%)
  blocking collectives  17.6 us (24%)
  local copies, waits for them, and re-layouts  5.49 us (8%)
  other arithmetic  3.4 us (5%)
  matrix products  2.78 us (4%)
    all_to_all x1, blocking collectives, body(): lax.all_to_all(spectra, 'inp', split_axis=0, concat_axis=3, tiled=True)  17.6 us
    all_to_all x1, waiting for transfers between devices, copy_for_each(): lax.all_to_all(jnp.broadcast_to(x[None], (devices, *x.shape)), axis, 0, 0...  14.3 us
    ppermute x1, waiting for transfers between devices, shifted(): return lax.ppermute(block, axis, route)  11 us
    all_to_all x1, starting transfers between devices, copy_for_each(): lax.all_to_all(jnp.broadcast_to(x[None], (devices, *x.shape)), axis, 0, 0...  10.1 us
    ppermute x1, starting transfers between devices, shifted(): return lax.ppermute(block, axis, route)  7.94 us
    dot_general x1, matrix products, body(): jnp.einsum('cpn,itn->ctpi', weights, filtered, precision=lax.Precision.HI...  1.75 us
  transfers between devices with their start and end apart: 2, of which 2 were waited for; matrix products, arithmetic and copies ran while one was open for 2% of the time, Pallas kernels for 0%

commit v1 on v0

v1 whole, which is shorter than its diff:
```python
import math

import jax
import jax.numpy as jnp
import numpy as np
from jax import lax
from jax.experimental import pallas as pl
from jax.experimental.pallas import tpu as pltpu
from jax.sharding import PartitionSpec as P

TAPS = 4
SAMPLES = 2048
CHANNELS = 32
CHAN_FIRST = 496
IN_BLK = 32
FR_BLK = 4
FRQ = 8
LANES = 128


def dft_table():
    bins = np.arange(CHANNELS, dtype=np.int64) + CHAN_FIRST
    turns = bins[:, None] * np.arange(SAMPLES, dtype=np.int64)[None, :] % SAMPLES
    phases = turns * (2.0 * math.pi / SAMPLES)
    both = np.concatenate([np.cos(phases), -np.sin(phases)]) / math.sqrt(SAMPLES)
    return both.astype(np.float32)


def two_terms(x):
    high = x.astype(jnp.bfloat16)
    low = (x - high.astype(jnp.float32)).astype(jnp.bfloat16)
    return high, low


def transform_kernel(first_ref, volt_ref, hist_ref, window_ref, table_ref, out_ref, rows_ref):
    volts = volt_ref[...].reshape(FR_BLK * IN_BLK, SAMPLES)
    hist = hist_ref[...].reshape((TAPS - 1) * IN_BLK, SAMPLES)
    frames = jnp.concatenate([volts, hist, jnp.zeros((IN_BLK, SAMPLES), jnp.bfloat16)], axis=0)
    table = table_ref[...]
    lane = lax.broadcasted_iota(jnp.int32, (2 * CHANNELS, LANES), 1)
    first = first_ref[0] == 0
    own = jnp.zeros((2 * CHANNELS, LANES), jnp.float32)
    later = own
    past = own
    for tap in range(TAPS):
        high, low = two_terms(table * window_ref[tap : tap + 1, :])
        dims = (((1,), (1,)), ((), ()))
        part = lax.dot_general(high, frames, dims, preferred_element_type=jnp.float32)
        part = part + lax.dot_general(low, frames, dims, preferred_element_type=jnp.float32)
        moved = part[:, :LANES]
        split = (TAPS - 1 - tap) * IN_BLK
        if split:
            moved = pltpu.roll(moved, split, 1)
            later = later + jnp.where(lane < split, moved, 0.0)
            moved = jnp.where(lane < split, 0.0, moved)
            before = part[:, LANES:]
            if tap:
                before = pltpu.roll(before, LANES - tap * IN_BLK, 1)
            past = past + jnp.where(lane < split, before, 0.0)
        own = own + moved
    own = own + jnp.where(first, past, 0.0)
    for part in range(2):
        rows = slice(part * CHANNELS, (part + 1) * CHANNELS)
        rows_ref[pl.ds(2 * part, CHANNELS, 4), :] = own[rows]
        rows_ref[pl.ds(2 * part + 1, CHANNELS, 4), :] = later[rows]
    chunk = rows_ref[...]
    for copy in range(FRQ):
        out_ref[copy] = chunk


def gram_kernel(tile_ref, got_ref, out_ref, by_tile_ref):
    lane_group = lax.broadcasted_iota(jnp.int32, (8, LANES), 1) // IN_BLK
    spectra = {}
    for blk in range(FRQ):
        for kind in range(4):
            quads = [got_ref[pl.ds(blk * LANES + 4 * jj + kind, 8, 16), :] for jj in range(4)]
            for slot in range(4 if kind % 2 == 0 else 3):
                row = None
                for jj in range(4):
                    shift = (jj - slot) % 4 * IN_BLK
                    moved = pltpu.roll(quads[jj], shift, 1) if shift else quads[jj]
                    row = moved if row is None else jnp.where(lane_group == jj, moved, row)
                spectra[blk, kind // 2, kind % 2, slot] = row
    for part in range(2):
        for blk in range(FRQ):
            for slot in range(4):
                row = spectra[blk, part, 0, slot]
                if blk and slot < TAPS - 1:
                    row = row + spectra[blk - 1, part, 1, slot]
                k = (part * FRQ + blk) * FR_BLK + slot
                by_tile_ref[pl.ds(8 * k, 8), :] = row
    half = FRQ * FR_BLK
    tile = tile_ref[0]
    left = by_tile_ref[pl.ds(tile, 2 * half, 8), :] * (1.0 / half)
    left = jnp.concatenate([left, jnp.concatenate([left[half:], -left[:half]], axis=0)], axis=1)
    high, low = two_terms(left)
    left = jnp.concatenate([high, high, low], axis=0)
    for col in range(8):
        high, low = two_terms(by_tile_ref[pl.ds(col, 2 * half, 8), :])
        right = jnp.concatenate([high, low, high], axis=0)
        vis = lax.dot_general(left, right, (((0,), (0,)), ((), ())), preferred_element_type=jnp.float32)
        for part in range(2):
            out_ref[pl.ds(2 * col + part, LANES, 16), :] = vis[part * LANES : (part + 1) * LANES]


def body(voltages, history, window):
    place = lax.axis_index("frq").astype(jnp.int32).reshape(1)
    smem = pl.BlockSpec(memory_space=pltpu.SMEM)
    vmem = pl.BlockSpec(memory_space=pltpu.VMEM)
    chunks = pl.pallas_call(
        transform_kernel,
        out_shape=jax.ShapeDtypeStruct((FRQ, LANES, LANES), jnp.float32),
        in_specs=[smem, vmem, vmem, vmem, vmem],
        out_specs=vmem,
        scratch_shapes=[pltpu.VMEM((LANES, LANES), jnp.float32)],
        name="transform",
    )(place, voltages.transpose(1, 0, 2), history.transpose(1, 0, 2), window, jnp.asarray(dft_table()))
    chunks = chunks.reshape(FRQ * CHANNELS, 4, LANES)
    got = lax.all_to_all(chunks, ("frq", "inp"), 0, 0, tiled=True)
    rows = pl.pallas_call(
        gram_kernel,
        out_shape=jax.ShapeDtypeStruct((LANES * 16, LANES), jnp.float32),
        in_specs=[smem, vmem],
        out_specs=vmem,
        scratch_shapes=[pltpu.VMEM((2 * FRQ * FR_BLK * 8, LANES), jnp.float32)],
        name="gram",
    )(place, got.reshape(FRQ * LANES, LANES))
    return rows.reshape(LANES, 8, 2, LANES).transpose(0, 2, 1, 3).reshape(LANES, 1, 2, 8 * LANES)


def solution(mesh):
    return jax.shard_map(
        body,
        mesh=mesh,
        in_specs=(P("inp", "frq", None), P("inp", None, None), P()),
        out_specs=P("frq", "inp", None, None),
        check_vma=False,
    )
```

time: 73.1 us -> 47.1 us (0.64)
  the two profiles are of different devices: /device:TPU:33 before, /device:TPU:1 now
where the time goes in v1:
time: 47.1 us; the launch traced here: 46.8 us
  blocking collectives  37 us (79%)
  Pallas kernels  7.7 us (16%)
  local copies, waits for them, and re-layouts  2.13 us (5%)
    all_to_all x1, blocking collectives, body(): got = lax.all_to_all(chunks, ('frq', 'inp'), 0, 0, tiled=True)  37 us
    pallas_call x1, Pallas kernels, body(): pl.pallas_call(transform_kernel, out_shape=jax.ShapeDtypeStruct((FRQ, LAN...  4.63 us
    pallas_call x1, Pallas kernels, body(): pl.pallas_call(gram_kernel, out_shape=jax.ShapeDtypeStruct((LANES * 16, L...  3.07 us
    unnamed x1, local copies, waits for them, and re-layouts  2.13 us

profile of v1, /device:TPU:1, one launch (start us, length us, event | category | flops | bytes accessed | tf_op | source)
XLA Modules:
  0.0 46.8 jit_solution(10694647867238190033)
XLA Ops:
  0.0 2.1 %copy.8 = bf16[32,4,2048]{2,0,1:T(8,128)(2,1)} copy(bf16[32,4,2048]{2,1,0:T(4,128)(2,1)} %param.4) | data formatting | bytes 1048576 | tf_op args[0]
  2.1 4.6 %transform.1 = f32[8,128,128]{2,1,0:T(8,128)} custom-call(s32[1]{0:T(128)} %bitcast.first_ref.tile_ref, bf16[4,32,2048]{2,1,0:T(8,128)(2,1)} %bitcast.13, bf16[3,32,2048]{2,1,0:T(8,128)(2,1)} %bitcast.15, f32[4,2048]{1,0:T(4,128)} %window_ref.1, f32[64,2048]{1,0:T(8,128)} %constant.6.clone.table_ref), custom_call_target="tpu_custom_call" | custom-call | tf_op jit(solution)/shard_map/transform/pallas_call | solution.py:110
  6.8 37.0 %all_to_all.5 = f32[256,4,128]{2,1,0:T(4,128)} all-to-all(f32[256,4,128]{2,1,0:T(4,128)} %bitcast.12), channel_id=1, replica_groups=mesh['inp'=32,'frq'=8] {'frq','inp'}, dimensions={0} | all-to-all | bytes 1048576 | tf_op jit(solution)/shard_map/all_to_all | solution.py:119
  43.7 3.1 %gram.1 = f32[2048,128]{1,0:T(8,128)} custom-call(s32[1]{0:T(128)} %bitcast.first_ref.tile_ref, f32[1024,128]{1,0:T(8,128)} %bitcast.14), custom_call_target="tpu_custom_call" | custom-call | tf_op jit(solution)/shard_map/gram/pallas_call | solution.py:120

commit v2 on v1

v2 whole, which is shorter than its diff:
```python
import math

import jax
import jax.numpy as jnp
import numpy as np
from jax import lax
from jax.experimental import pallas as pl
from jax.experimental.pallas import tpu as pltpu
from jax.sharding import PartitionSpec as P

TAPS = 4
SAMPLES = 2048
CHANNELS = 32
CHAN_FIRST = 496
IN_BLK = 32
FR_BLK = 4
FRQ = 8
LANES = 128
STEP = 256
STEPS = SAMPLES // STEP
POWER = 16
TOP = 7


def dft_table():
    bins = np.arange(CHANNELS, dtype=np.int64) + CHAN_FIRST
    turns = bins[:, None] * np.arange(SAMPLES, dtype=np.int64)[None, :] % SAMPLES
    phases = turns * (2.0 * math.pi / SAMPLES)
    both = np.concatenate([np.cos(phases), -np.sin(phases)]) / math.sqrt(SAMPLES)
    return both.astype(np.float32)


def two_terms(x):
    high = x.astype(jnp.bfloat16)
    low = (x - high.astype(jnp.float32)).astype(jnp.bfloat16)
    return high, low


def transform_kernel(first_ref, volt_hbm, hist_hbm, window_ref, table_hbm, out_ref,
                     volt_ref, hist_ref, table_ref, rows_ref, sems):
    copies = []
    for step in range(STEPS):
        cols = pl.ds(step * STEP, STEP)
        moves = [(table_hbm.at[:, cols], table_ref.at[:, cols]), (hist_hbm.at[:, cols], hist_ref.at[:, cols])]
        for tile in range(step * STEP // LANES, (step + 1) * STEP // LANES):
            moves.append((volt_hbm.at[:, :, pl.ds(tile * LANES, LANES)], volt_ref.at[tile]))
        copies.append([pltpu.make_async_copy(*move, sems.at[step, i]) for i, move in enumerate(moves)])
        for copy in copies[-1]:
            copy.start()
    lane = lax.broadcasted_iota(jnp.int32, (2 * CHANNELS, LANES), 1)
    frame = lane % FR_BLK
    zeros = jnp.zeros((IN_BLK, STEP), jnp.bfloat16)
    dims = (((1,), (1,)), ((), ()))
    total = None
    for step in range(STEPS):
        for copy in copies[step]:
            copy.wait()
        cols = slice(step * STEP, (step + 1) * STEP)
        tiles = range(step * STEP // LANES, (step + 1) * STEP // LANES)
        volts = jnp.concatenate([volt_ref.at[tile].reshape(LANES, LANES)[...] for tile in tiles], axis=1)
        frames = jnp.concatenate([volts, hist_ref[:, cols], zeros], axis=0)
        table = table_ref[:, cols]
        weights = jnp.concatenate([table * window_ref[tap : tap + 1, cols] for tap in range(TAPS)], axis=0)
        high, low = two_terms(weights)
        part = lax.dot_general(high, frames, dims, preferred_element_type=jnp.float32)
        part = part + lax.dot_general(low, frames, dims, preferred_element_type=jnp.float32)
        total = part if total is None else total + part
    own = jnp.zeros((2 * CHANNELS, LANES), jnp.float32)
    later = own
    past = own
    for tap in range(TAPS):
        part = total[tap * 2 * CHANNELS : (tap + 1) * 2 * CHANNELS]
        here = part[:, :LANES]
        moved = TAPS - 1 - tap
        if moved == 0:
            own = own + here
            continue
        own = own + jnp.where(frame < moved, 0.0, pltpu.roll(here, moved, 1))
        later = later + jnp.where(frame < moved, pltpu.roll(here, LANES - FR_BLK + moved, 1), 0.0)
        before = part[:, LANES:]
        if tap:
            before = pltpu.roll(before, LANES - tap * IN_BLK, 1)
        past = past + jnp.where(lane < moved * IN_BLK, before, 0.0)
    row = lax.broadcasted_iota(jnp.int32, (LANES, LANES), 0)
    col = lax.broadcasted_iota(jnp.int32, (LANES, LANES), 1)
    order = jnp.where(col == row % FR_BLK * IN_BLK + row // FR_BLK, 1.0, 0.0).astype(jnp.bfloat16)
    high, low = two_terms(jnp.concatenate([own, later], axis=0))
    sorted_rows = jnp.dot(high, order, preferred_element_type=jnp.float32)
    sorted_rows = sorted_rows + jnp.dot(low, order, preferred_element_type=jnp.float32)
    own = sorted_rows[: 2 * CHANNELS] + jnp.where(first_ref[0] == 0, past, 0.0)
    later = sorted_rows[2 * CHANNELS :]
    quads = [own[:CHANNELS], later[:CHANNELS], own[CHANNELS:], later[CHANNELS:]]
    top = jnp.maximum(jnp.maximum(jnp.abs(quads[0]), jnp.abs(quads[1])), jnp.maximum(jnp.abs(quads[2]), jnp.abs(quads[3])))
    top = jnp.maximum(jnp.max(top, axis=1, keepdims=True), 2.0**-100)
    shift = jnp.broadcast_to(jnp.ceil(jnp.log2(top)) - TOP, (CHANNELS, LANES))
    factor = jnp.exp2(-shift)
    lane = lane[:CHANNELS]
    for kind in range(4):
        value = quads[kind] * factor
        power = value * value
        power = power * power
        power = power * power
        power = power * power
        value = jnp.where(value < 0.0, -power, power)
        if kind % 2:
            value = jnp.where(lane < (TAPS - 1) * IN_BLK, value, shift)
        rows_ref[pl.ds(kind, CHANNELS, 4), :] = value
    chunk = rows_ref[...].astype(jnp.bfloat16)
    for copy in range(FRQ):
        out_ref[copy] = chunk


def gram_kernel(tile_ref, got_ref, out_ref, wide_ref, by_tile_ref):
    wide_ref[...] = got_ref[...].astype(jnp.float32)
    lane_group = lax.broadcasted_iota(jnp.int32, (8, LANES), 1) // IN_BLK
    spectra = {}
    for blk in range(FRQ):
        quads = [[wide_ref[pl.ds(blk * LANES + 4 * jj + kind, 8, 16), :] for kind in range(4)] for jj in range(4)]
        for jj in range(4):
            shift = jnp.broadcast_to(quads[jj][1][:, LANES - 1 :], (8, LANES))
            for kind in range(4):
                code = quads[jj][kind]
                value = jnp.exp2(jnp.log2(jnp.abs(code)) * (1.0 / POWER) + shift)
                quads[jj][kind] = jnp.where(code < 0.0, -value, value)
        for kind in range(4):
            for slot in range(4 if kind % 2 == 0 else 3):
                row = None
                for jj in range(4):
                    shift = (jj - slot) % 4 * IN_BLK
                    moved = pltpu.roll(quads[jj][kind], shift, 1) if shift else quads[jj][kind]
                    row = moved if row is None else jnp.where(lane_group == jj, moved, row)
                spectra[blk, kind // 2, kind % 2, slot] = row
    for part in range(2):
        for blk in range(FRQ):
            for slot in range(4):
                row = spectra[blk, part, 0, slot]
                if blk and slot < TAPS - 1:
                    row = row + spectra[blk - 1, part, 1, slot]
                k = (part * FRQ + blk) * FR_BLK + slot
                by_tile_ref[pl.ds(8 * k, 8), :] = row
    half = FRQ * FR_BLK
    tile = tile_ref[0]
    left = by_tile_ref[pl.ds(tile, 2 * half, 8), :] * (1.0 / half)
    left = jnp.concatenate([left, jnp.concatenate([left[half:], -left[:half]], axis=0)], axis=1)
    high, low = two_terms(left)
    left = jnp.concatenate([high, high, low], axis=0)
    for col in range(8):
        high, low = two_terms(by_tile_ref[pl.ds(col, 2 * half, 8), :])
        right = jnp.concatenate([high, low, high], axis=0)
        vis = lax.dot_general(left, right, (((0,), (0,)), ((), ())), preferred_element_type=jnp.float32)
        for part in range(2):
            out_ref[pl.ds(2 * col + part, LANES, 16), :] = vis[part * LANES : (part + 1) * LANES]


def body(voltages, history, window):
    place = lax.axis_index("frq").astype(jnp.int32).reshape(1)
    smem = pl.BlockSpec(memory_space=pltpu.SMEM)
    vmem = pl.BlockSpec(memory_space=pltpu.VMEM)
    hbm = pl.BlockSpec(memory_space=pl.ANY)
    past = history.transpose(1, 0, 2).reshape((TAPS - 1) * IN_BLK, SAMPLES)
    chunks = pl.pallas_call(
        transform_kernel,
        out_shape=jax.ShapeDtypeStruct((FRQ, LANES, LANES), jnp.bfloat16),
        in_specs=[smem, hbm, hbm, vmem, hbm],
        out_specs=vmem,
        scratch_shapes=[
            pltpu.VMEM((SAMPLES // LANES, IN_BLK, FR_BLK, LANES), jnp.bfloat16),
            pltpu.VMEM(past.shape, jnp.bfloat16),
            pltpu.VMEM((2 * CHANNELS, SAMPLES), jnp.float32),
            pltpu.VMEM((LANES, LANES), jnp.float32),
            pltpu.SemaphoreType.DMA((STEPS, 2 + STEP // LANES)),
        ],
        name="transform",
    )(place, voltages, past, window, jnp.asarray(dft_table()))
    chunks = chunks.reshape(FRQ * CHANNELS, 4, LANES)
    got = lax.all_to_all(chunks, ("frq", "inp"), 0, 0, tiled=True)
    rows = pl.pallas_call(
        gram_kernel,
        out_shape=jax.ShapeDtypeStruct((LANES * 16, LANES), jnp.float32),
        in_specs=[smem, vmem],
        out_specs=vmem,
        scratch_shapes=[
            pltpu.VMEM((FRQ * LANES, LANES), jnp.float32),
            pltpu.VMEM((2 * FRQ * FR_BLK * 8, LANES), jnp.float32),
        ],
        name="gram",
    )(place, got.reshape(FRQ * LANES, LANES))
    return rows.reshape(LANES, 8, 2, LANES).transpose(0, 2, 1, 3).reshape(LANES, 1, 2, 8 * LANES)


def solution(mesh):
    return jax.shard_map(
        body,
        mesh=mesh,
        in_specs=(P("inp", "frq", None), P("inp", None, None), P()),
        out_specs=P("frq", "inp", None, None),
        check_vma=False,
    )
```

time: 47.1 us -> 40.1 us (0.85)
  blocking collectives: 37 us -> 31.4 us
  local copies, waits for them, and re-layouts: 2.13 us -> 0 us
  Pallas kernels: 7.7 us -> 8.48 us
    all_to_all x1, blocking collectives: 37 us -> 31.4 us  [body(): got = lax.all_to_all(chunks, ('frq', 'inp'), 0, 0, tiled=True)]
    unnamed x1 -> x0, local copies, waits for them, and re-layouts: 2.13 us -> none
    pallas_call x1, Pallas kernels: 4.63 us -> 5.4 us  [body(): pl.pallas_call(transform_kernel, out_shape=jax.ShapeDtypeStruct((FRQ, LAN...]
where the time goes in v2:
time: 40.1 us; the launch traced here: 39.9 us
  blocking collectives  31.4 us (78%)
  Pallas kernels  8.48 us (21%)
    all_to_all x1, blocking collectives, body(): got = lax.all_to_all(chunks, ('frq', 'inp'), 0, 0, tiled=True)  31.4 us
    pallas_call x1, Pallas kernels, body(): pl.pallas_call(transform_kernel, out_shape=jax.ShapeDtypeStruct((FRQ, LAN...  5.4 us
    pallas_call x1, Pallas kernels, body(): pl.pallas_call(gram_kernel, out_shape=jax.ShapeDtypeStruct((LANES * 16, L...  3.08 us

profile of v2, /device:TPU:1, one launch (start us, length us, event | category | flops | bytes accessed | tf_op | source)
XLA Modules:
  0.0 39.9 jit_solution(15689546268842002481)
XLA Ops:
  0.0 5.4 %transform.1 = bf16[8,128,128]{2,1,0:T(8,128)(2,1)} custom-call(s32[1]{0:T(128)} %bitcast.first_ref.tile_ref, bf16[32,4,2048]{2,1,0:T(4,128)(2,1)} %volt_hbm.1, bf16[96,2048]{1,0:T(8,128)(2,1)} %bitcast.13, f32[4,2048]{1,0:T(4,128)} %window_ref.1, f32[64,2048]{1,0:T(8,128)} %constant.6.clone.table_hbm), custom_call_target="tpu_custom_call" | custom-call | tf_op jit(solution)/shard_map/transform/pallas_call | solution.py:161
  5.4 31.4 %all_to_all.5 = bf16[256,4,128]{2,1,0:T(4,128)(2,1)} all-to-all(bf16[256,4,128]{2,1,0:T(4,128)(2,1)} %bitcast.12), channel_id=1, replica_groups=mesh['inp'=32,'frq'=8] {'frq','inp'}, dimensions={0} | all-to-all | bytes 524288 | tf_op jit(solution)/shard_map/all_to_all | solution.py:176
  36.8 3.1 %gram.1 = f32[2048,128]{1,0:T(8,128)} custom-call(s32[1]{0:T(128)} %bitcast.first_ref.tile_ref, bf16[1024,128]{1,0:T(8,128)(2,1)} %bitcast.11), custom_call_target="tpu_custom_call" | custom-call | tf_op jit(solution)/shard_map/gram/pallas_call | solution.py:177

commit v3 on v2

--- a/solution.py
+++ b/solution.py
@@ -16,7 +16,7 @@
 FR_BLK = 4
 FRQ = 8
 LANES = 128
-STEP = 256
+STEP = 2048
 STEPS = SAMPLES // STEP
 POWER = 16
 TOP = 7
@@ -160,7 +160,7 @@
     past = history.transpose(1, 0, 2).reshape((TAPS - 1) * IN_BLK, SAMPLES)
     chunks = pl.pallas_call(
         transform_kernel,
-        out_shape=jax.ShapeDtypeStruct((FRQ, LANES, LANES), jnp.bfloat16),
+        out_shape=pltpu.VMEM((FRQ, LANES, LANES), jnp.bfloat16),
         in_specs=[smem, hbm, hbm, vmem, hbm],
         out_specs=vmem,
         scratch_shapes=[
@@ -184,7 +184,7 @@
             pltpu.VMEM((2 * FRQ * FR_BLK * 8, LANES), jnp.float32),
         ],
         name="gram",
-    )(place, got.reshape(FRQ * LANES, LANES))
+    )(place, pltpu.with_memory_space_constraint(got.reshape(FRQ * LANES, LANES), pltpu.VMEM))
     return rows.reshape(LANES, 8, 2, LANES).transpose(0, 2, 1, 3).reshape(LANES, 1, 2, 8 * LANES)
 
 

time: 40.1 us -> 36.7 us (0.915)
  Pallas kernels: 8.48 us -> 5.39 us
    pallas_call x1, Pallas kernels: 5.4 us -> 3.27 us  [body(): pl.pallas_call(transform_kernel, out_shape=pltpu.VMEM((FRQ, LANES, LANES)...]
    pallas_call x1, Pallas kernels: 3.08 us -> 2.13 us  [body(): pl.pallas_call(gram_kernel, out_shape=jax.ShapeDtypeStruct((LANES * 16, L...]
where the time goes in v3:
time: 36.7 us; the launch traced here: 36.5 us
  blocking collectives  31.1 us (85%)
  Pallas kernels  5.39 us (15%)
    all_to_all x1, blocking collectives, body(): got = lax.all_to_all(chunks, ('frq', 'inp'), 0, 0, tiled=True)  31.1 us
    pallas_call x1, Pallas kernels, body(): pl.pallas_call(transform_kernel, out_shape=pltpu.VMEM((FRQ, LANES, LANES)...  3.27 us
    pallas_call x1, Pallas kernels, body(): pl.pallas_call(gram_kernel, out_shape=jax.ShapeDtypeStruct((LANES * 16, L...  2.13 us

profile of v3, /device:TPU:1, one launch (start us, length us, event | category | flops | bytes accessed | tf_op | source)
XLA Modules:
  0.0 36.5 jit_solution(16345725517267184799)
XLA Ops:
  0.0 3.3 %transform.1 = bf16[8,128,128]{2,1,0:T(8,128)(2,1)S(1)} custom-call(s32[1]{0:T(128)} %bitcast.first_ref.tile_ref, bf16[32,4,2048]{2,1,0:T(4,128)(2,1)} %volt_hbm.1, bf16[96,2048]{1,0:T(8,128)(2,1)} %bitcast.13, f32[4,2048]{1,0:T(4,128)} %window_ref.1, f32[64,2048]{1,0:T(8,128)} %constant.6.clone.table_hbm), custom_call_target="tpu_custom_call" | custom-call | tf_op jit(solution)/shard_map/transform/pallas_call | solution.py:161
  3.3 31.1 %all_to_all.5 = bf16[256,4,128]{2,1,0:T(4,128)(2,1)S(1)} all-to-all(bf16[256,4,128]{2,1,0:T(4,128)(2,1)S(1)} %bitcast.12), channel_id=1, replica_groups=mesh['inp'=32,'frq'=8] {'frq','inp'}, dimensions={0} | all-to-all | bytes 524288 | tf_op jit(solution)/shard_map/all_to_all | solution.py:176
  34.3 2.1 %gram.1 = f32[2048,128]{1,0:T(8,128)} custom-call(s32[1]{0:T(128)} %bitcast.first_ref.tile_ref, bf16[1024,128]{1,0:T(8,128)(2,1)S(1)} %bitcast.11), custom_call_target="tpu_custom_call" | custom-call | tf_op jit(solution)/shard_map/gram/pallas_call | solution.py:177

commit v4 on v2

v4 whole, which is shorter than its diff:
```python
import math

import jax
import jax.numpy as jnp
import numpy as np
from jax import lax
from jax.experimental import pallas as pl
from jax.experimental.pallas import tpu as pltpu
from jax.sharding import PartitionSpec as P

TAPS = 4
SAMPLES = 2048
CHANNELS = 32
CHAN_FIRST = 496
IN_BLK = 32
FR_BLK = 4
FRQ = 8
LANES = 128
STEP = 256
POWER = 16
TOP = 7


def dft_table():
    bins = np.arange(CHANNELS, dtype=np.int64) + CHAN_FIRST
    turns = bins[:, None] * np.arange(SAMPLES, dtype=np.int64)[None, :] % SAMPLES
    phases = turns * (2.0 * math.pi / SAMPLES)
    both = np.concatenate([np.cos(phases), -np.sin(phases)]) / math.sqrt(SAMPLES)
    return both.astype(np.float32)


def two_terms(x):
    high = x.astype(jnp.bfloat16)
    low = (x - high.astype(jnp.float32)).astype(jnp.bfloat16)
    return high, low


def transform_kernel(volt_hbm, hist_hbm, window_hbm, table_hbm, out_ref,
                     volt_ref, hist_ref, window_ref, table_ref, rows_ref, sems):
    tiles = SAMPLES // LANES
    pltpu.make_async_copy(window_hbm, window_ref, sems.at[0]).start()
    pltpu.make_async_copy(table_hbm, table_ref, sems.at[1]).start()
    for tile in range(tiles):
        pltpu.make_async_copy(volt_hbm.at[:, :, pl.ds(tile * LANES, LANES)], volt_ref.at[tile], sems.at[2]).start()
    pltpu.make_async_copy(hist_hbm, hist_ref, sems.at[3]).start()
    pltpu.make_async_copy(window_hbm, window_ref, sems.at[0]).wait()
    pltpu.make_async_copy(table_hbm, table_ref, sems.at[1]).wait()
    pltpu.make_async_copy(volt_ref, volt_ref, sems.at[2]).wait()
    pltpu.make_async_copy(hist_hbm, hist_ref, sems.at[3]).wait()
    lane = lax.broadcasted_iota(jnp.int32, (2 * CHANNELS, LANES), 1)
    frame = lane % FR_BLK
    zeros = jnp.zeros((IN_BLK, STEP), jnp.bfloat16)
    dims = (((1,), (1,)), ((), ()))
    total = None
    for step in range(SAMPLES // STEP):
        cols = slice(step * STEP, (step + 1) * STEP)
        span = range(step * STEP // LANES, (step + 1) * STEP // LANES)
        volts = jnp.concatenate([volt_ref.at[tile].reshape(LANES, LANES)[...] for tile in span], axis=1)
        frames = jnp.concatenate([volts, hist_ref[:, cols], zeros], axis=0)
        table = table_ref[:, cols]
        weights = jnp.concatenate([table * window_ref[tap : tap + 1, cols] for tap in range(TAPS)], axis=0)
        high, low = two_terms(weights)
        part = lax.dot_general(high, frames, dims, preferred_element_type=jnp.float32)
        part = part + lax.dot_general(low, frames, dims, preferred_element_type=jnp.float32)
        total = part if total is None else total + part
    own = jnp.zeros((2 * CHANNELS, LANES), jnp.float32)
    later = own
    past = own
    for tap in range(TAPS):
        part = total[tap * 2 * CHANNELS : (tap + 1) * 2 * CHANNELS]
        here = part[:, :LANES]
        moved = TAPS - 1 - tap
        if moved == 0:
            own = own + here
            continue
        own = own + jnp.where(frame < moved, 0.0, pltpu.roll(here, moved, 1))
        later = later + jnp.where(frame < moved, pltpu.roll(here, LANES - FR_BLK + moved, 1), 0.0)
        before = part[:, LANES:]
        if tap:
            before = pltpu.roll(before, LANES - tap * IN_BLK, 1)
        past = past + jnp.where(lane < moved * IN_BLK, before, 0.0)
    row = lax.broadcasted_iota(jnp.int32, (LANES, LANES), 0)
    col = lax.broadcasted_iota(jnp.int32, (LANES, LANES), 1)
    order = jnp.where(col == row % FR_BLK * IN_BLK + row // FR_BLK, 1.0, 0.0).astype(jnp.bfloat16)
    high, low = two_terms(jnp.concatenate([own, later], axis=0))
    sorted_rows = jnp.dot(high, order, preferred_element_type=jnp.float32)
    sorted_rows = sorted_rows + jnp.dot(low, order, preferred_element_type=jnp.float32)
    own = sorted_rows[: 2 * CHANNELS] + jnp.where(lax.axis_index("frq") == 0, past, 0.0)
    later = sorted_rows[2 * CHANNELS :]
    quads = [own[:CHANNELS], own[CHANNELS:], later[:CHANNELS], later[CHANNELS:]]
    top = jnp.maximum(jnp.maximum(jnp.abs(quads[0]), jnp.abs(quads[1])), jnp.maximum(jnp.abs(quads[2]), jnp.abs(quads[3])))
    top = jnp.maximum(jnp.max(top, axis=1, keepdims=True), 2.0**-100)
    shift = jnp.broadcast_to(jnp.ceil(jnp.log2(top)) - TOP, (CHANNELS, LANES))
    factor = jnp.exp2(-shift)
    lane = lane[:CHANNELS]
    for kind in range(4):
        value = quads[kind] * factor
        power = value * value
        power = power * power
        power = power * power
        power = power * power
        value = jnp.where(value < 0.0, -power, power)
        if kind >= 2:
            value = jnp.where(lane < (TAPS - 1) * IN_BLK, value, shift)
        value = pltpu.roll(value, lax.axis_index("inp") % 4 * IN_BLK, 1)
        for copy in range(2):
            rows_ref[pl.ds(4 * copy + kind, CHANNELS, 8), :] = value
    for chan in range(CHANNELS):
        twice = rows_ref[8 * chan : 8 * chan + 8, :]
        chunk = jnp.concatenate([twice, twice], axis=0).astype(jnp.bfloat16)
        for copy in range(FRQ // 4):
            out_ref[pl.ds(4 * FRQ * chan + 16 * copy, 16), :] = chunk


def frames_of(got_ref, first_row):
    rows = 4 * FRQ
    lane_group = lax.broadcasted_iota(jnp.int32, (rows, LANES), 1) // IN_BLK
    row = lax.broadcasted_iota(jnp.int32, (rows, LANES), 0)
    upper = row % 4 >= 2
    quarters = [got_ref[pl.ds(first_row + rows * g, rows), :].astype(jnp.float32) for g in range(4)]
    codes = []
    for slot in range(4):
        code = quarters[-slot % 4]
        for group in range(1, 4):
            code = jnp.where(lane_group == group, quarters[(group - slot) % 4], code)
        codes.append(pltpu.roll(code, LANES - slot * IN_BLK, 1) if slot else code)
    shift = jnp.where(upper, codes[3], pltpu.roll(codes[3], rows - 2, 0))
    values = []
    for slot in range(4):
        value = jnp.exp2(jnp.log2(jnp.abs(codes[slot])) * (1.0 / POWER) + shift)
        value = jnp.where(codes[slot] < 0.0, -value, value)
        if slot < TAPS - 1:
            value = value + jnp.where(row < 2, 0.0, pltpu.roll(value, 2, 0))
        values.append(value)
    pairs = [jnp.where(upper, pltpu.roll(values[i + 1], 2, 0), values[i]) for i in (0, 2)]
    return jnp.concatenate(pairs, axis=0)


def gram_kernel(got_ref, out_hbm, vis_ref, sems):
    left = frames_of(got_ref, lax.axis_index("frq") * LANES) * (1.0 / (FRQ * FR_BLK))
    real = lax.broadcasted_iota(jnp.int32, left.shape, 0) % 2 == 0
    turned = jnp.where(real, pltpu.roll(left, left.shape[0] - 1, 0), -pltpu.roll(left, 1, 0))
    high, low = two_terms(jnp.concatenate([left, turned], axis=1))
    left = jnp.concatenate([high, high, low], axis=0)
    row = lax.broadcasted_iota(jnp.int32, (2 * LANES, 2 * LANES), 0)
    col = lax.broadcasted_iota(jnp.int32, (2 * LANES, 2 * LANES), 1)
    order = jnp.where(col == row % 2 * LANES + row // 2, 1.0, 0.0).astype(jnp.bfloat16)
    left = lax.dot_general(order, left, (((1,), (1,)), ((), ())), preferred_element_type=jnp.float32)
    left = left.astype(jnp.bfloat16)
    copies = []
    for pair in range(4):
        high, low = two_terms(jnp.concatenate([frames_of(got_ref, (2 * pair + i) * LANES) for i in range(2)], axis=1))
        right = jnp.concatenate([high, low, high], axis=0)
        vis = jnp.dot(left, right, preferred_element_type=jnp.float32)
        for i in range(2):
            tile = 2 * pair + i
            vis_ref.at[tile].reshape(2 * LANES, LANES)[...] = vis[:, i * LANES : (i + 1) * LANES]
            copies.append(pltpu.make_async_copy(vis_ref.at[tile], out_hbm.at[:, tile], sems.at[tile]))
            copies[-1].start()
    for copy in copies:
        copy.wait()


def body(voltages, history, window):
    vmem = pl.BlockSpec(memory_space=pltpu.VMEM)
    hbm = pl.BlockSpec(memory_space=pl.ANY)
    past = history.transpose(1, 0, 2).reshape((TAPS - 1) * IN_BLK, SAMPLES)
    chunks = pl.pallas_call(
        transform_kernel,
        out_shape=pltpu.VMEM((FRQ * LANES, LANES), jnp.bfloat16),
        in_specs=[hbm] * 4,
        out_specs=vmem,
        scratch_shapes=[
            pltpu.VMEM((SAMPLES // LANES, IN_BLK, FR_BLK, LANES), jnp.bfloat16),
            pltpu.VMEM(past.shape, jnp.bfloat16),
            pltpu.VMEM(window.shape, jnp.float32),
            pltpu.VMEM((2 * CHANNELS, SAMPLES), jnp.float32),
            pltpu.VMEM((2 * LANES, LANES), jnp.float32),
            pltpu.SemaphoreType.DMA((4,)),
        ],
        name="transform",
    )(voltages, past, window, jnp.asarray(dft_table()))
    chunks = chunks.reshape(FRQ * CHANNELS, 4, LANES)
    got = lax.all_to_all(chunks, ("inp", "frq"), 0, 0, tiled=True)
    got = pltpu.with_memory_space_constraint(got.reshape(FRQ * LANES, LANES), pltpu.VMEM)
    tiles = pl.pallas_call(
        gram_kernel,
        out_shape=jax.ShapeDtypeStruct((LANES, 8, 2, LANES), jnp.float32),
        in_specs=[vmem],
        out_specs=hbm,
        scratch_shapes=[pltpu.VMEM((8, LANES, 2, LANES), jnp.float32), pltpu.SemaphoreType.DMA((8,))],
        name="gram",
    )(got)
    return tiles.transpose(0, 2, 1, 3).reshape(LANES, 1, 2, 8 * LANES)


def solution(mesh):
    return jax.shard_map(
        body,
        mesh=mesh,
        in_specs=(P("inp", "frq", None), P("inp", None, None), P()),
        out_specs=P("frq", "inp", None, None),
        check_vma=False,
    )
```

time: 40.1 us -> 35.6 us (0.89)
  Pallas kernels: 8.48 us -> 4.33 us
    pallas_call x2, Pallas kernels: 8.48 us -> 4.33 us  [the longest x1 2.61 us: body(): pl.pallas_call(transform_kernel, out_shape=pltpu.VMEM((FRQ * LANES, LANES...]
where the time goes in v4:
time: 35.6 us; the launch traced here: 35.5 us
  blocking collectives  31.1 us (87%)
  Pallas kernels  4.33 us (12%)
    all_to_all x1, blocking collectives, body(): got = lax.all_to_all(chunks, ('inp', 'frq'), 0, 0, tiled=True)  31.1 us
    pallas_call x1, Pallas kernels, body(): pl.pallas_call(transform_kernel, out_shape=pltpu.VMEM((FRQ * LANES, LANES...  2.61 us
    pallas_call x1, Pallas kernels, body(): pl.pallas_call(gram_kernel, out_shape=jax.ShapeDtypeStruct((LANES, 8, 2,...  1.72 us

profile of v4, /device:TPU:1, one launch (start us, length us, event | category | flops | bytes accessed | tf_op | source)
XLA Modules:
  0.0 35.5 jit_solution(4672299400490651141)
XLA Ops:
  0.0 2.6 %transform.1 = bf16[1024,128]{1,0:T(8,128)(2,1)S(1)} custom-call(bf16[32,4,2048]{2,1,0:T(4,128)(2,1)} %volt_hbm.1, bf16[96,2048]{1,0:T(8,128)(2,1)} %bitcast.10, f32[4,2048]{1,0:T(4,128)} %window_hbm.1, f32[64,2048]{1,0:T(8,128)} %constant.2.clone.table_hbm), custom_call_target="tpu_custom_call" | custom-call | tf_op jit(solution)/shard_map/transform/pallas_call | solution.py:168
  2.6 31.1 %all_to_all.5 = bf16[256,4,128]{2,1,0:T(4,128)(2,1)S(1)} all-to-all(bf16[256,4,128]{2,1,0:T(4,128)(2,1)S(1)} %bitcast.9), channel_id=1, replica_groups=mesh['inp'=32,'frq'=8] {'inp','frq'}, dimensions={0} | all-to-all | bytes 524288 | tf_op jit(solution)/shard_map/all_to_all | solution.py:184
  33.8 1.7 %gram.1 = f32[128,8,2,128]{3,2,1,0:T(2,128)} custom-call(bf16[1024,128]{1,0:T(8,128)(2,1)S(1)} %bitcast.8), custom_call_target="tpu_custom_call" | custom-call | tf_op jit(solution)/shard_map/gram/pallas_call | solution.py:186

commit v5 on v4

v5 whole, which is shorter than its diff:
```python
import math

import jax
import jax.numpy as jnp
import numpy as np
from jax import lax
from jax.experimental import pallas as pl
from jax.experimental.pallas import tpu as pltpu
from jax.sharding import PartitionSpec as P

TAPS = 4
SAMPLES = 2048
CHANNELS = 32
CHAN_FIRST = 496
IN_BLK = 32
FR_BLK = 4
FRQ = 8
LANES = 128
STEP = 256
POWER = 16
TOP = 7


def dft_table():
    bins = np.arange(CHANNELS, dtype=np.int64) + CHAN_FIRST
    turns = bins[:, None] * np.arange(SAMPLES, dtype=np.int64)[None, :] % SAMPLES
    phases = turns * (2.0 * math.pi / SAMPLES)
    both = np.concatenate([np.cos(phases), -np.sin(phases)]) / math.sqrt(SAMPLES)
    return both.astype(np.float32)


def two_terms(x):
    high = x.astype(jnp.bfloat16)
    low = (x - high.astype(jnp.float32)).astype(jnp.bfloat16)
    return high, low


def products(table_ref, window_ref, taps, frames_at):
    dims = (((1,), (1,)), ((), ()))
    total = None
    for step in range(SAMPLES // STEP):
        cols = slice(step * STEP, (step + 1) * STEP)
        table = table_ref[:, cols]
        weights = jnp.concatenate([table * window_ref[tap : tap + 1, cols] for tap in range(taps)], axis=0)
        high, low = two_terms(weights)
        frames = frames_at(step)
        part = lax.dot_general(high, frames, dims, preferred_element_type=jnp.float32)
        part = part + lax.dot_general(low, frames, dims, preferred_element_type=jnp.float32)
        total = part if total is None else total + part
    return [total[tap * 2 * CHANNELS : (tap + 1) * 2 * CHANNELS] for tap in range(taps)]


def transform_kernel(volt_hbm, hist_hbm, window_hbm, table_hbm, out_ref,
                     volt_ref, hist_ref, window_ref, table_ref, rows_ref, past_ref, sems):
    first = (lax.axis_index("y") == 0) & (lax.axis_index("zh") == 0)
    hist_copy = pltpu.make_async_copy(hist_hbm, hist_ref, sems.at[3])
    pltpu.make_async_copy(window_hbm, window_ref, sems.at[0]).start()
    pltpu.make_async_copy(table_hbm, table_ref, sems.at[1]).start()
    for tile in range(SAMPLES // LANES):
        pltpu.make_async_copy(volt_hbm.at[:, :, pl.ds(tile * LANES, LANES)], volt_ref.at[tile], sems.at[2]).start()
    lane = lax.broadcasted_iota(jnp.int32, (2 * CHANNELS, LANES), 1)
    past_ref[...] = jnp.zeros((2 * CHANNELS, LANES), jnp.float32)
    pltpu.make_async_copy(window_hbm, window_ref, sems.at[0]).wait()
    pltpu.make_async_copy(table_hbm, table_ref, sems.at[1]).wait()

    @pl.when(first)
    def _():
        hist_copy.start()
        hist_copy.wait()

        def frames_at(step):
            rows = hist_ref[:, step * STEP : (step + 1) * STEP]
            return jnp.concatenate([rows, jnp.zeros((IN_BLK, STEP), jnp.bfloat16)], axis=0)

        past = jnp.zeros((2 * CHANNELS, LANES), jnp.float32)
        for tap, before in enumerate(products(table_ref, window_ref, TAPS - 1, frames_at)):
            if tap:
                before = pltpu.roll(before, LANES - tap * IN_BLK, 1)
            past = past + jnp.where(lane < (TAPS - 1 - tap) * IN_BLK, before, 0.0)
        past_ref[...] = past

    pltpu.make_async_copy(volt_ref, volt_ref, sems.at[2]).wait()

    def frames_at(step):
        tiles = range(step * STEP // LANES, (step + 1) * STEP // LANES)
        return jnp.concatenate([volt_ref.at[tile].reshape(LANES, LANES)[...] for tile in tiles], axis=1)

    frame = lane % FR_BLK
    own = later = None
    for tap, here in enumerate(products(table_ref, window_ref, TAPS, frames_at)):
        moved = TAPS - 1 - tap
        if moved == 0:
            own = own + here
            continue
        kept = jnp.where(frame < moved, 0.0, pltpu.roll(here, moved, 1))
        passed = jnp.where(frame < moved, pltpu.roll(here, LANES - FR_BLK + moved, 1), 0.0)
        own = kept if own is None else own + kept
        later = passed if later is None else later + passed
    past = past_ref[...]
    top = jnp.maximum(jnp.maximum(jnp.abs(own), jnp.abs(later)), jnp.abs(past))
    top = jnp.maximum(top[:CHANNELS], top[CHANNELS:])
    top = jnp.maximum(jnp.max(top, axis=1, keepdims=True), 2.0**-100)
    shift = jnp.broadcast_to(jnp.ceil(jnp.log2(top)) - (TOP - 1), (CHANNELS, LANES))
    factor = jnp.exp2(-shift)
    row = lax.broadcasted_iota(jnp.int32, (LANES, LANES), 0)
    col = lax.broadcasted_iota(jnp.int32, (LANES, LANES), 1)
    order = jnp.where(col == row % FR_BLK * IN_BLK + row // FR_BLK, 1.0, 0.0).astype(jnp.bfloat16)
    high, low = two_terms(jnp.concatenate([own, later], axis=0))
    sorted_rows = jnp.dot(high, order, preferred_element_type=jnp.float32)
    sorted_rows = sorted_rows + jnp.dot(low, order, preferred_element_type=jnp.float32)
    own = sorted_rows[: 2 * CHANNELS] + past
    later = sorted_rows[2 * CHANNELS :]
    quads = [own[:CHANNELS], own[CHANNELS:], later[:CHANNELS], later[CHANNELS:]]
    lane = lane[:CHANNELS]
    for kind in range(4):
        value = quads[kind] * factor
        power = value * value
        power = power * power
        power = power * power
        power = power * power
        value = jnp.where(value < 0.0, -power, power)
        if kind >= 2:
            value = jnp.where(lane < (TAPS - 1) * IN_BLK, value, shift)
        value = pltpu.roll(value, (lax.axis_index("zl") % 2 * 2 + lax.axis_index("c")) * IN_BLK, 1)
        for copy in range(2):
            rows_ref[pl.ds(4 * copy + kind, CHANNELS, 8), :] = value
    out_ref[...] = rows_ref[...].astype(jnp.bfloat16)


def frames_of(blocks, tile):
    rows = 4 * FRQ
    lane_group = lax.broadcasted_iota(jnp.int32, (8, LANES), 1) // IN_BLK
    row = lax.broadcasted_iota(jnp.int32, (rows, LANES), 0)
    start = 8 * (3 - lax.axis_index("y"))
    nothing_before = (row >= start) & (row < start + 2)
    upper = row % 4 >= 2
    quarters = [[ref[pl.ds((4 * tile + g) * 8, 8), :] for ref in blocks] for g in range(4)]
    codes = []
    for slot in range(4):
        code = list(quarters[-slot % 4])
        for group in range(1, 4):
            source = quarters[(group - slot) % 4]
            code = [jnp.where(lane_group == group, source[i], code[i]) for i in range(4)]
        code = jnp.concatenate([piece.astype(jnp.float32) for piece in code], axis=0)
        codes.append(pltpu.roll(code, LANES - slot * IN_BLK, 1) if slot else code)
    shift = jnp.where(upper, codes[3], pltpu.roll(codes[3], rows - 2, 0))
    values = []
    for slot in range(4):
        value = jnp.exp2(jnp.log2(jnp.abs(codes[slot])) * (1.0 / POWER) + shift)
        value = jnp.where(codes[slot] < 0.0, -value, value)
        if slot < TAPS - 1:
            value = value + jnp.where(nothing_before, 0.0, pltpu.roll(value, 2, 0))
        values.append(value)
    pairs = [jnp.where(upper, pltpu.roll(values[i + 1], 2, 0), values[i]) for i in (0, 2)]
    return jnp.concatenate(pairs, axis=0)


def gram_kernel(b0_ref, b1_ref, b2_ref, b3_ref, out_hbm, vis_ref, sems):
    blocks = (b0_ref, b1_ref, b2_ref, b3_ref)
    left = frames_of(blocks, 2 * lax.axis_index("y") + lax.axis_index("zh")) * (1.0 / (FRQ * FR_BLK))
    real = lax.broadcasted_iota(jnp.int32, left.shape, 0) % 2 == 0
    turned = jnp.where(real, pltpu.roll(left, left.shape[0] - 1, 0), -pltpu.roll(left, 1, 0))
    high, low = two_terms(jnp.concatenate([left, turned], axis=1))
    left = jnp.concatenate([high, high, low], axis=0)
    row = lax.broadcasted_iota(jnp.int32, (2 * LANES, 2 * LANES), 0)
    col = lax.broadcasted_iota(jnp.int32, (2 * LANES, 2 * LANES), 1)
    order = jnp.where(col == row % 2 * LANES + row // 2, 1.0, 0.0).astype(jnp.bfloat16)
    left = lax.dot_general(order, left, (((1,), (1,)), ((), ())), preferred_element_type=jnp.float32)
    left = left.astype(jnp.bfloat16)
    copies = []
    for pair in range(4):
        high, low = two_terms(jnp.concatenate([frames_of(blocks, 2 * pair + i) for i in range(2)], axis=1))
        right = jnp.concatenate([high, low, high], axis=0)
        vis = jnp.dot(left, right, preferred_element_type=jnp.float32)
        for i in range(2):
            tile = 2 * pair + i
            vis_ref.at[tile].reshape(2 * LANES, LANES)[...] = vis[:, i * LANES : (i + 1) * LANES]
            copies.append(pltpu.make_async_copy(vis_ref.at[tile], out_hbm.at[:, tile], sems.at[tile]))
            copies[-1].start()
    for copy in copies:
        copy.wait()


def body(voltages, history, window):
    vmem = pl.BlockSpec(memory_space=pltpu.VMEM)
    hbm = pl.BlockSpec(memory_space=pl.ANY)
    past = history.transpose(1, 0, 2).reshape((TAPS - 1) * IN_BLK, SAMPLES)
    chunks = pl.pallas_call(
        transform_kernel,
        out_shape=pltpu.VMEM((2 * LANES, LANES), jnp.bfloat16),
        in_specs=[hbm] * 4,
        out_specs=vmem,
        scratch_shapes=[
            pltpu.VMEM((SAMPLES // LANES, IN_BLK, FR_BLK, LANES), jnp.bfloat16),
            pltpu.VMEM(past.shape, jnp.bfloat16),
            pltpu.VMEM(window.shape, jnp.float32),
            pltpu.VMEM((2 * CHANNELS, SAMPLES), jnp.float32),
            pltpu.VMEM((2 * LANES, LANES), jnp.float32),
            pltpu.VMEM((2 * CHANNELS, LANES), jnp.float32),
            pltpu.SemaphoreType.DMA((4,)),
        ],
        name="transform",
    )(voltages, past, window, jnp.asarray(dft_table()))
    chunks = chunks.reshape(2 * CHANNELS, 4, LANES)
    mine = lax.all_to_all(chunks, ("x", "zl", "c", "zh"), 0, 0, tiled=True).reshape(2 * LANES, LANES)
    ahead, behind, across = (lax.ppermute(mine, "y", [(i, (i + k) % 4) for i in range(4)]) for k in (1, 3, 2))
    blocks = [pltpu.with_memory_space_constraint(x, pltpu.VMEM) for x in (behind, across, ahead, mine)]
    tiles = pl.pallas_call(
        gram_kernel,
        out_shape=jax.ShapeDtypeStruct((LANES, 8, 2, LANES), jnp.float32),
        in_specs=[vmem] * 4,
        out_specs=hbm,
        scratch_shapes=[pltpu.VMEM((8, LANES, 2, LANES), jnp.float32), pltpu.SemaphoreType.DMA((8,))],
        name="gram",
    )(*blocks)
    return tiles.transpose(0, 2, 1, 3).reshape(LANES, 1, 2, 8 * LANES)


def solution(mesh):
    fine = jax.sharding.Mesh(mesh.devices.reshape(4, 4, 2, 4, 2), ("x", "zl", "c", "y", "zh"))
    inp, frq = ("x", "zl", "c"), ("y", "zh")
    return jax.shard_map(
        body,
        mesh=fine,
        in_specs=(P(inp, frq, None), P(inp, None, None), P()),
        out_specs=P(frq, inp, None, None),
        check_vma=False,
    )
```

time: 35.6 us -> 34.2 us (0.961)
  blocking collectives: 31.1 us -> 21.1 us
  starting transfers between devices: 0 us -> 4.98 us
  waiting for transfers between devices: 0 us -> 2.34 us
  Pallas kernels: 4.33 us -> 5.51 us
    all_to_all x1, blocking collectives: 31.1 us -> 21.1 us  [body(): lax.all_to_all(chunks, ('x', 'zl', 'c', 'zh'), 0, 0, tiled=True)]
    ppermute x0 -> x3, starting transfers between devices: none -> 4.98 us  [body(): lax.ppermute(mine, 'y', [(i, (i + k) % 4) for i in range(4)])]
    ppermute x0 -> x3, waiting for transfers between devices: none -> 2.34 us  [body(): lax.ppermute(mine, 'y', [(i, (i + k) % 4) for i in range(4)])]
    pallas_call x1, Pallas kernels: 2.61 us -> 3.8 us  [body(): pl.pallas_call(transform_kernel, out_shape=pltpu.VMEM((2 * LANES, LANES),...]
  transfers between devices with their start and end apart: 0 -> 3, of which waited for: 0 -> 2; matrix products, arithmetic and copies ran while one was open for 0% -> 0% of each run, Pallas kernels for 0% -> 0%
where the time goes in v5:
time: 34.2 us; the launch traced here: 33.9 us
  blocking collectives  21.1 us (62%)
  Pallas kernels  5.51 us (16%)
  starting transfers between devices  4.98 us (15%)
  waiting for transfers between devices  2.34 us (7%)
    all_to_all x1, blocking collectives, body(): lax.all_to_all(chunks, ('x', 'zl', 'c', 'zh'), 0, 0, tiled=True)  21.1 us
    ppermute x3, starting transfers between devices, body(): lax.ppermute(mine, 'y', [(i, (i + k) % 4) for i in range(4)])  4.98 us
    pallas_call x1, Pallas kernels, body(): pl.pallas_call(transform_kernel, out_shape=pltpu.VMEM((2 * LANES, LANES),...  3.8 us
    ppermute x3, waiting for transfers between devices, body(): lax.ppermute(mine, 'y', [(i, (i + k) % 4) for i in range(4)])  2.34 us
    pallas_call x1, Pallas kernels, body(): pl.pallas_call(gram_kernel, out_shape=jax.ShapeDtypeStruct((LANES, 8, 2,...  1.72 us
  transfers between devices with their start and end apart: 3, of which 2 were waited for; matrix products, arithmetic and copies ran while one was open for 0% of the time, Pallas kernels for 0%

profile of v5, /device:TPU:1, one launch (start us, length us, event | category | flops | bytes accessed | tf_op | source)
XLA Modules:
  0.0 33.9 jit_solution(2444992960358930408)
XLA Ops:
  0.0 3.8 %transform.1 = bf16[256,128]{1,0:T(8,128)(2,1)S(1)} custom-call(bf16[32,4,2048]{2,1,0:T(4,128)(2,1)} %volt_hbm.1, bf16[96,2048]{1,0:T(8,128)(2,1)} %bitcast.13, f32[4,2048]{1,0:T(4,128)} %window_hbm.1, f32[64,2048]{1,0:T(8,128)} %constant.2.clone.table_hbm), custom_call_target="tpu_custom_call" | custom-call | tf_op jit(solution)/shard_map/transform/pallas_call | solution.py:188
  3.8 21.1 %all_to_all.5 = bf16[64,4,128]{2,1,0:T(4,128)(2,1)S(1)} all-to-all(bf16[64,4,128]{2,1,0:T(4,128)(2,1)S(1)} %bitcast.12), channel_id=1, replica_groups=mesh['x'=4,'zl'=4,'c'=2,'y'=4,'zh'=2] {'x','zl','c','zh'}, dimensions={0} | all-to-all | bytes 131072 | tf_op jit(solution)/shard_map/all_to_all | solution.py:205
  24.9 1.3 %collective-permute-start.2 = (bf16[256,128]{1,0:T(8,128)(2,1)S(1)}, bf16[256,128]{1,0:T(8,128)(2,1)S(1)}, u32[]{:S(2)}, u32[]{:S(2)}) collective-permute-start(bf16[256,128]{1,0:T(8,128)(2,1)S(1)} %bitcast.8), channel_id=1, source_target_pairs={{0,2},{2,4},{4,6},{6,0},{1,3},{3,5},{5,7},{7,1},{8,10},{10,12},{12... | collective-permute-start | bytes 196616 | tf_op jit(solution)/shard_map/ppermute | solution.py:206
  26.2 2.6 %collective-permute-start.1 = (bf16[256,128]{1,0:T(8,128)(2,1)S(1)}, bf16[256,128]{1,0:T(8,128)(2,1)S(1)}, u32[]{:S(2)}, u32[]{:S(2)}) collective-permute-start(bf16[256,128]{1,0:T(8,128)(2,1)S(1)} %bitcast.9), channel_id=1, source_target_pairs={{0,4},{2,6},{4,0},{6,2},{1,5},{3,7},{5,1},{7,3},{8,12},{10,14},{12... | collective-permute-start | bytes 196616 | tf_op jit(solution)/shard_map/ppermute | solution.py:206
  28.8 1.1 %collective-permute-start = (bf16[256,128]{1,0:T(8,128)(2,1)S(1)}, bf16[256,128]{1,0:T(8,128)(2,1)S(1)}, u32[]{:S(2)}, u32[]{:S(2)}) collective-permute-start(bf16[256,128]{1,0:T(8,128)(2,1)S(1)} %bitcast.10), channel_id=1, source_target_pairs={{0,6},{2,0},{4,2},{6,4},{1,7},{3,1},{5,3},{7,5},{8,14},{10,8},{12,... | collective-permute-start | bytes 196616 | tf_op jit(solution)/shard_map/ppermute | solution.py:206
  29.8 0.0 collective-permute-done.2.b2_ref
  29.9 1.5 %collective-permute-done.1.b1_ref = bf16[256,128]{1,0:T(8,128)(2,1)S(1)} collective-permute-done((bf16[256,128]{1,0:T(8,128)(2,1)S(1)}, bf16[256,128]{1,0:T(8,128)(2,1)S(1)}, u32[]{:S(2)}, u32[]{:S(2)}) %collective-permute-start.1) | collective-permute-done | bytes 65568 | tf_op jit(solution)/shard_map/ppermute | solution.py:206
  31.4 0.8 %collective-permute-done.b0_ref = bf16[256,128]{1,0:T(8,128)(2,1)S(1)} collective-permute-done((bf16[256,128]{1,0:T(8,128)(2,1)S(1)}, bf16[256,128]{1,0:T(8,128)(2,1)S(1)}, u32[]{:S(2)}, u32[]{:S(2)}) %collective-permute-start) | collective-permute-done | bytes 65568 | tf_op jit(solution)/shard_map/ppermute | solution.py:206
  32.2 1.7 %gram.1 = f32[128,8,2,128]{3,2,1,0:T(2,128)} custom-call(bf16[256,128]{1,0:T(8,128)(2,1)S(1)} %collective-permute-done.b0_ref, bf16[256,128]{1,0:T(8,128)(2,1)S(1)} %collective-permute-done.1.b1_ref, bf16[256,128]{1,0:T(8,128)(2,1)S(1)} %collective-permute-done.2.b2_ref, bf16[256,128]{1,0:T(8,128)(2,1)S(1)} %bitcast.11), custom_call_target="tpu_custom_call" | custom-call | tf_op jit(solution)/shard_map/gram/pallas_call | solution.py:208
Async XLA Ops:
  24.9 5.0 %collective-permute-start.2 = (bf16[256,128]{1,0:T(8,128)(2,1)S(1)}, bf16[256,128]{1,0:T(8,128)(2,1)S(1)}, u32[]{:S(2)}, u32[]{:S(2)}) collective-permute-start(bf16[256,128]{1,0:T(8,128)(2,1)S(1)} %bitcast.8), channel_id=1, source_target_pairs={{0,2},{2,4},{4,6},{6,0},{1,3},{3,5},{5,7},{7,1},{8,10},{10,12},{12... | collective-permute-start | bytes 196616 | tf_op jit(solution)/shard_map/ppermute | solution.py:206
  26.2 5.2 %collective-permute-start.1 = (bf16[256,128]{1,0:T(8,128)(2,1)S(1)}, bf16[256,128]{1,0:T(8,128)(2,1)S(1)}, u32[]{:S(2)}, u32[]{:S(2)}) collective-permute-start(bf16[256,128]{1,0:T(8,128)(2,1)S(1)} %bitcast.9), channel_id=1, source_target_pairs={{0,4},{2,6},{4,0},{6,2},{1,5},{3,7},{5,1},{7,3},{8,12},{10,14},{12... | collective-permute-start | bytes 196616 | tf_op jit(solution)/shard_map/ppermute | solution.py:206
  28.8 3.4 %collective-permute-start = (bf16[256,128]{1,0:T(8,128)(2,1)S(1)}, bf16[256,128]{1,0:T(8,128)(2,1)S(1)}, u32[]{:S(2)}, u32[]{:S(2)}) collective-permute-start(bf16[256,128]{1,0:T(8,128)(2,1)S(1)} %bitcast.10), channel_id=1, source_target_pairs={{0,6},{2,0},{4,2},{6,4},{1,7},{3,1},{5,3},{7,5},{8,14},{10,8},{12,... | collective-permute-start | bytes 196616 | tf_op jit(solution)/shard_map/ppermute | solution.py:206

commit v6 on v5

--- a/solution.py
+++ b/solution.py
@@ -21,12 +21,12 @@
 TOP = 7
 
 
-def dft_table():
+def dft_start():
     bins = np.arange(CHANNELS, dtype=np.int64) + CHAN_FIRST
-    turns = bins[:, None] * np.arange(SAMPLES, dtype=np.int64)[None, :] % SAMPLES
-    phases = turns * (2.0 * math.pi / SAMPLES)
-    both = np.concatenate([np.cos(phases), -np.sin(phases)]) / math.sqrt(SAMPLES)
-    return both.astype(np.float32)
+    turns = bins[:, None] * np.arange(LANES, dtype=np.int64)[None, :] % SAMPLES
+    begin = np.exp(turns * (-2j * math.pi / SAMPLES)) / math.sqrt(SAMPLES)
+    turn = np.exp(bins[:, None] * LANES % SAMPLES * (-2j * math.pi / SAMPLES)) * np.ones((1, LANES))
+    return np.concatenate([begin.real, begin.imag, turn.real, turn.imag]).astype(np.float32)
 
 
 def two_terms(x):
@@ -35,12 +35,17 @@
     return high, low
 
 
-def products(table_ref, window_ref, taps, frames_at):
+def products(start_ref, window_ref, taps, frames_at):
     dims = (((1,), (1,)), ((), ()))
     total = None
+    real, imag, turn_real, turn_imag = (start_ref[part * CHANNELS : (part + 1) * CHANNELS, :] for part in range(4))
     for step in range(SAMPLES // STEP):
         cols = slice(step * STEP, (step + 1) * STEP)
-        table = table_ref[:, cols]
+        table = []
+        for _ in range(STEP // LANES):
+            table.append(jnp.concatenate([real, imag], axis=0))
+            real, imag = real * turn_real - imag * turn_imag, real * turn_imag + imag * turn_real
+        table = jnp.concatenate(table, axis=1)
         weights = jnp.concatenate([table * window_ref[tap : tap + 1, cols] for tap in range(taps)], axis=0)
         high, low = two_terms(weights)
         frames = frames_at(step)
@@ -50,18 +55,18 @@
     return [total[tap * 2 * CHANNELS : (tap + 1) * 2 * CHANNELS] for tap in range(taps)]
 
 
-def transform_kernel(volt_hbm, hist_hbm, window_hbm, table_hbm, out_ref,
-                     volt_ref, hist_ref, window_ref, table_ref, rows_ref, past_ref, sems):
+def transform_kernel(volt_hbm, hist_hbm, window_hbm, start_hbm, out_ref,
+                     volt_ref, hist_ref, window_ref, start_ref, rows_ref, past_ref, sems):
     first = (lax.axis_index("y") == 0) & (lax.axis_index("zh") == 0)
     hist_copy = pltpu.make_async_copy(hist_hbm, hist_ref, sems.at[3])
     pltpu.make_async_copy(window_hbm, window_ref, sems.at[0]).start()
-    pltpu.make_async_copy(table_hbm, table_ref, sems.at[1]).start()
+    pltpu.make_async_copy(start_hbm, start_ref, sems.at[1]).start()
     for tile in range(SAMPLES // LANES):
         pltpu.make_async_copy(volt_hbm.at[:, :, pl.ds(tile * LANES, LANES)], volt_ref.at[tile], sems.at[2]).start()
     lane = lax.broadcasted_iota(jnp.int32, (2 * CHANNELS, LANES), 1)
     past_ref[...] = jnp.zeros((2 * CHANNELS, LANES), jnp.float32)
     pltpu.make_async_copy(window_hbm, window_ref, sems.at[0]).wait()
-    pltpu.make_async_copy(table_hbm, table_ref, sems.at[1]).wait()
+    pltpu.make_async_copy(start_hbm, start_ref, sems.at[1]).wait()
 
     @pl.when(first)
     def _():
@@ -73,7 +78,7 @@
             return jnp.concatenate([rows, jnp.zeros((IN_BLK, STEP), jnp.bfloat16)], axis=0)
 
         past = jnp.zeros((2 * CHANNELS, LANES), jnp.float32)
-        for tap, before in enumerate(products(table_ref, window_ref, TAPS - 1, frames_at)):
+        for tap, before in enumerate(products(start_ref, window_ref, TAPS - 1, frames_at)):
             if tap:
                 before = pltpu.roll(before, LANES - tap * IN_BLK, 1)
             past = past + jnp.where(lane < (TAPS - 1 - tap) * IN_BLK, before, 0.0)
@@ -87,7 +92,7 @@
 
     frame = lane % FR_BLK
     own = later = None
-    for tap, here in enumerate(products(table_ref, window_ref, TAPS, frames_at)):
+    for tap, here in enumerate(products(start_ref, window_ref, TAPS, frames_at)):
         moved = TAPS - 1 - tap
         if moved == 0:
             own = own + here
@@ -96,6 +101,8 @@
         passed = jnp.where(frame < moved, pltpu.roll(here, LANES - FR_BLK + moved, 1), 0.0)
         own = kept if own is None else own + kept
         later = passed if later is None else later + passed
+    last = (lax.axis_index("y") == 3) & (lax.axis_index("zh") == 1)
+    later = jnp.where(last, 0.0, later)
     past = past_ref[...]
     top = jnp.maximum(jnp.maximum(jnp.abs(own), jnp.abs(later)), jnp.abs(past))
     top = jnp.maximum(top[:CHANNELS], top[CHANNELS:])
@@ -127,37 +134,40 @@
     out_ref[...] = rows_ref[...].astype(jnp.bfloat16)
 
 
-def frames_of(blocks, tile):
-    rows = 4 * FRQ
+def decode_kernel(got_ref, sums_ref, passed_ref):
     lane_group = lax.broadcasted_iota(jnp.int32, (8, LANES), 1) // IN_BLK
-    row = lax.broadcasted_iota(jnp.int32, (rows, LANES), 0)
-    start = 8 * (3 - lax.axis_index("y"))
-    nothing_before = (row >= start) & (row < start + 2)
+    row = lax.broadcasted_iota(jnp.int32, (8, LANES), 0)
     upper = row % 4 >= 2
-    quarters = [[ref[pl.ds((4 * tile + g) * 8, 8), :] for ref in blocks] for g in range(4)]
-    codes = []
-    for slot in range(4):
-        code = list(quarters[-slot % 4])
-        for group in range(1, 4):
-            source = quarters[(group - slot) % 4]
-            code = [jnp.where(lane_group == group, source[i], code[i]) for i in range(4)]
-        code = jnp.concatenate([piece.astype(jnp.float32) for piece in code], axis=0)
-        codes.append(pltpu.roll(code, LANES - slot * IN_BLK, 1) if slot else code)
-    shift = jnp.where(upper, codes[3], pltpu.roll(codes[3], rows - 2, 0))
-    values = []
-    for slot in range(4):
-        value = jnp.exp2(jnp.log2(jnp.abs(codes[slot])) * (1.0 / POWER) + shift)
-        value = jnp.where(codes[slot] < 0.0, -value, value)
-        if slot < TAPS - 1:
-            value = value + jnp.where(nothing_before, 0.0, pltpu.roll(value, 2, 0))
-        values.append(value)
-    pairs = [jnp.where(upper, pltpu.roll(values[i + 1], 2, 0), values[i]) for i in (0, 2)]
-    return jnp.concatenate(pairs, axis=0)
-
-
-def gram_kernel(b0_ref, b1_ref, b2_ref, b3_ref, out_hbm, vis_ref, sems):
-    blocks = (b0_ref, b1_ref, b2_ref, b3_ref)
-    left = frames_of(blocks, 2 * lax.axis_index("y") + lax.axis_index("zh")) * (1.0 / (FRQ * FR_BLK))
+    for tile in range(8):
+        quarters = [got_ref[pl.ds((4 * tile + g) * 8, 8), :].astype(jnp.float32) for g in range(4)]
+        halves = [jnp.where(lane_group < 2, quarters[-slot % 4], quarters[(2 - slot) % 4]) for slot in range(4)]
+        codes = [jnp.where(lane_group % 2 == 0, halves[slot], halves[slot - 1]) for slot in range(4)]
+        codes = [pltpu.roll(code, (-slot % 4) * IN_BLK, 1) if slot else code for slot, code in enumerate(codes)]
+        shift = jnp.where(upper, codes[3], pltpu.roll(codes[3], 6, 0))
+        values = []
+        moved = []
+        for code in codes:
+            size = jnp.maximum(jnp.abs(code), 2.0**-126)
+            values.append(code * jnp.exp2(jnp.log2(size) * (1.0 / POWER - 1.0) + shift))
+        for slot in range(TAPS - 1):
+            moved.append(pltpu.roll(values[slot], 2, 0))
+            values[slot] = values[slot] + jnp.where(row >= 4, moved[slot], 0.0)
+        for pair in range(2):
+            rows = pl.ds(8 * pair, 8)
+            sums_ref[tile, rows, :] = jnp.where(upper, pltpu.roll(values[2 * pair + 1], 2, 0), values[2 * pair])
+        second = jnp.where(row < 4, pltpu.roll(moved[1], 2, 0), 0.0)
+        passed_ref[tile, :8, :] = jnp.where(row < 2, moved[0], second)
+        passed_ref[tile, 8:, :] = jnp.where(row < 2, moved[2], 0.0)
+
+
+def gram_kernel(*refs):
+    sums_refs, passed_refs, out_hbm, vis_ref, sems = refs[:4], refs[4:8], *refs[8:]
+
+    def frames_of(tile):
+        return jnp.concatenate([sums_refs[i][tile] + passed_refs[i - 1][tile] for i in range(4)], axis=0)
+
+    tile = 2 * lax.axis_index("y") + lax.axis_index("zh")
+    left = frames_of(tile) * (1.0 / (FRQ * FR_BLK))
     real = lax.broadcasted_iota(jnp.int32, left.shape, 0) % 2 == 0
     turned = jnp.where(real, pltpu.roll(left, left.shape[0] - 1, 0), -pltpu.roll(left, 1, 0))
     high, low = two_terms(jnp.concatenate([left, turned], axis=1))
@@ -169,7 +179,7 @@
     left = left.astype(jnp.bfloat16)
     copies = []
     for pair in range(4):
-        high, low = two_terms(jnp.concatenate([frames_of(blocks, 2 * pair + i) for i in range(2)], axis=1))
+        high, low = two_terms(jnp.concatenate([frames_of(2 * pair + i) for i in range(2)], axis=1))
         right = jnp.concatenate([high, low, high], axis=0)
         vis = jnp.dot(left, right, preferred_element_type=jnp.float32)
         for i in range(2):
@@ -194,25 +204,35 @@
             pltpu.VMEM((SAMPLES // LANES, IN_BLK, FR_BLK, LANES), jnp.bfloat16),
             pltpu.VMEM(past.shape, jnp.bfloat16),
             pltpu.VMEM(window.shape, jnp.float32),
-            pltpu.VMEM((2 * CHANNELS, SAMPLES), jnp.float32),
+            pltpu.VMEM((4 * CHANNELS, LANES), jnp.float32),
             pltpu.VMEM((2 * LANES, LANES), jnp.float32),
             pltpu.VMEM((2 * CHANNELS, LANES), jnp.float32),
             pltpu.SemaphoreType.DMA((4,)),
         ],
         name="transform",
-    )(voltages, past, window, jnp.asarray(dft_table()))
+    )(voltages, past, window, jnp.asarray(dft_start()))
     chunks = chunks.reshape(2 * CHANNELS, 4, LANES)
     mine = lax.all_to_all(chunks, ("x", "zl", "c", "zh"), 0, 0, tiled=True).reshape(2 * LANES, LANES)
     ahead, behind, across = (lax.ppermute(mine, "y", [(i, (i + k) % 4) for i in range(4)]) for k in (1, 3, 2))
-    blocks = [pltpu.with_memory_space_constraint(x, pltpu.VMEM) for x in (behind, across, ahead, mine)]
+    sums, passed = [], []
+    for i, piece in enumerate((behind, across, ahead, mine)):
+        found = pl.pallas_call(
+            decode_kernel,
+            out_shape=[pltpu.VMEM((8, 2 * 8, LANES), jnp.float32)] * 2,
+            in_specs=[vmem],
+            out_specs=[vmem] * 2,
+            name=f"decode{i}",
+        )(pltpu.with_memory_space_constraint(piece, pltpu.VMEM))
+        sums.append(pltpu.with_memory_space_constraint(found[0], pltpu.VMEM))
+        passed.append(pltpu.with_memory_space_constraint(found[1], pltpu.VMEM))
     tiles = pl.pallas_call(
         gram_kernel,
         out_shape=jax.ShapeDtypeStruct((LANES, 8, 2, LANES), jnp.float32),
-        in_specs=[vmem] * 4,
+        in_specs=[vmem] * 8,
         out_specs=hbm,
         scratch_shapes=[pltpu.VMEM((8, LANES, 2, LANES), jnp.float32), pltpu.SemaphoreType.DMA((8,))],
         name="gram",
-    )(*blocks)
+    )(*sums, *passed)
     return tiles.transpose(0, 2, 1, 3).reshape(LANES, 1, 2, 8 * LANES)
 
 

time: 34.2 us -> 34 us (level)
  waiting for transfers between devices: 2.34 us -> 1.91 us
    pallas_call x0 -> x4, Pallas kernels: none -> 0.56 us  [body(): pl.pallas_call(decode_kernel, out_shape=[pltpu.VMEM((8, 2 * 8, LANES), jn...]
    ppermute x3, waiting for transfers between devices: 2.34 us -> 1.91 us  [body(): lax.ppermute(mine, 'y', [(i, (i + k) % 4) for i in range(4)])]
  transfers between devices with their start and end apart: 3 -> 3, of which waited for: 2 -> 2; matrix products, arithmetic and copies ran while one was open for 0% -> 0% of each run, Pallas kernels for 0% -> 1%
where the time goes in v6:
time: 34 us; the launch traced here: 33.7 us
  blocking collectives  21.1 us (62%)
  Pallas kernels  5.65 us (17%)
  starting transfers between devices  4.98 us (15%)
  waiting for transfers between devices  1.91 us (6%)
    all_to_all x1, blocking collectives, body(): lax.all_to_all(chunks, ('x', 'zl', 'c', 'zh'), 0, 0, tiled=True)  21.1 us
    ppermute x3, starting transfers between devices, body(): lax.ppermute(mine, 'y', [(i, (i + k) % 4) for i in range(4)])  4.98 us
    pallas_call x1, Pallas kernels, body(): pl.pallas_call(transform_kernel, out_shape=pltpu.VMEM((2 * LANES, LANES),...  3.66 us
    ppermute x3, waiting for transfers between devices, body(): lax.ppermute(mine, 'y', [(i, (i + k) % 4) for i in range(4)])  1.91 us
    pallas_call x1, Pallas kernels, body(): pl.pallas_call(gram_kernel, out_shape=jax.ShapeDtypeStruct((LANES, 8, 2,...  1.42 us
  transfers between devices with their start and end apart: 3, of which 2 were waited for; matrix products, arithmetic and copies ran while one was open for 0% of the time, Pallas kernels for 1%

profile of v6, /device:TPU:1, one launch (start us, length us, event | category | flops | bytes accessed | tf_op | source)
XLA Modules:
  0.0 33.7 jit_solution(6233922131208489995)
XLA Ops:
  0.0 3.7 %transform.1 = bf16[256,128]{1,0:T(8,128)(2,1)S(1)} custom-call(bf16[32,4,2048]{2,1,0:T(4,128)(2,1)} %volt_hbm.1, bf16[96,2048]{1,0:T(8,128)(2,1)} %bitcast.13, f32[4,2048]{1,0:T(4,128)} %window_hbm.1, f32[128,128]{1,0:T(8,128)} %constant.2.clone.start_hbm), custom_call_target="tpu_custom_call" | custom-call | tf_op jit(solution)/shard_map/transform/pallas_call | solution.py:198
  3.7 21.1 %all_to_all.5 = bf16[64,4,128]{2,1,0:T(4,128)(2,1)S(1)} all-to-all(bf16[64,4,128]{2,1,0:T(4,128)(2,1)S(1)} %bitcast.8), channel_id=1, replica_groups=mesh['x'=4,'zl'=4,'c'=2,'y'=4,'zh'=2] {'x','zl','c','zh'}, dimensions={0} | all-to-all | bytes 131072 | tf_op jit(solution)/shard_map/all_to_all | solution.py:215
  24.8 1.3 %collective-permute-start.2 = (bf16[256,128]{1,0:T(8,128)(2,1)S(1)}, bf16[256,128]{1,0:T(8,128)(2,1)S(1)}, u32[]{:S(2)}, u32[]{:S(2)}) collective-permute-start(bf16[256,128]{1,0:T(8,128)(2,1)S(1)} %bitcast.9), channel_id=1, source_target_pairs={{0,2},{2,4},{4,6},{6,0},{1,3},{3,5},{5,7},{7,1},{8,10},{10,12},{12... | collective-permute-start | bytes 196616 | tf_op jit(solution)/shard_map/ppermute | solution.py:216
  26.1 2.6 %collective-permute-start.1 = (bf16[256,128]{1,0:T(8,128)(2,1)S(1)}, bf16[256,128]{1,0:T(8,128)(2,1)S(1)}, u32[]{:S(2)}, u32[]{:S(2)}) collective-permute-start(bf16[256,128]{1,0:T(8,128)(2,1)S(1)} %bitcast.10), channel_id=1, source_target_pairs={{0,4},{2,6},{4,0},{6,2},{1,5},{3,7},{5,1},{7,3},{8,12},{10,14},{12... | collective-permute-start | bytes 196616 | tf_op jit(solution)/shard_map/ppermute | solution.py:216
  28.7 1.1 %collective-permute-start = (bf16[256,128]{1,0:T(8,128)(2,1)S(1)}, bf16[256,128]{1,0:T(8,128)(2,1)S(1)}, u32[]{:S(2)}, u32[]{:S(2)}) collective-permute-start(bf16[256,128]{1,0:T(8,128)(2,1)S(1)} %bitcast.11), channel_id=1, source_target_pairs={{0,6},{2,0},{4,2},{6,4},{1,7},{3,1},{5,3},{7,5},{8,14},{10,8},{12,... | collective-permute-start | bytes 196616 | tf_op jit(solution)/shard_map/ppermute | solution.py:216
  29.8 0.1 decode3.1
  29.9 0.0 collective-permute-done.2.got_ref
  29.9 0.1 decode2.1
  30.1 1.2 %collective-permute-done.1.got_ref = bf16[256,128]{1,0:T(8,128)(2,1)S(1)} collective-permute-done((bf16[256,128]{1,0:T(8,128)(2,1)S(1)}, bf16[256,128]{1,0:T(8,128)(2,1)S(1)}, u32[]{:S(2)}, u32[]{:S(2)}) %collective-permute-start.1) | collective-permute-done | bytes 65568 | tf_op jit(solution)/shard_map/ppermute | solution.py:216
  31.3 0.1 decode1.1
  31.5 0.7 %collective-permute-done.got_ref = bf16[256,128]{1,0:T(8,128)(2,1)S(1)} collective-permute-done((bf16[256,128]{1,0:T(8,128)(2,1)S(1)}, bf16[256,128]{1,0:T(8,128)(2,1)S(1)}, u32[]{:S(2)}, u32[]{:S(2)}) %collective-permute-start) | collective-permute-done | bytes 65568 | tf_op jit(solution)/shard_map/ppermute | solution.py:216
  32.1 0.1 decode0.1
  32.3 1.4 %gram.1 = f32[128,8,2,128]{3,2,1,0:T(2,128)} custom-call(f32[8,16,128]{2,1,0:T(8,128)S(1)} %get-tuple-element.13.refs_0_, f32[8,16,128]{2,1,0:T(8,128)S(1)} %get-tuple-element.14.refs_1_, f32[8,16,128]{2,1,0:T(8,128)S(1)} %get-tuple-element.15.refs_2_, f32[8,16,128]{2,1,0:T(8,128)S(1)} %get-tuple-element.16.refs_3_, ...), custom_call_target="tpu_custom_call" | custom-call | tf_op jit(solution)/shard_map/gram/pallas_call | solution.py:228
Async XLA Ops:
  24.8 5.1 %collective-permute-start.2 = (bf16[256,128]{1,0:T(8,128)(2,1)S(1)}, bf16[256,128]{1,0:T(8,128)(2,1)S(1)}, u32[]{:S(2)}, u32[]{:S(2)}) collective-permute-start(bf16[256,128]{1,0:T(8,128)(2,1)S(1)} %bitcast.9), channel_id=1, source_target_pairs={{0,2},{2,4},{4,6},{6,0},{1,3},{3,5},{5,7},{7,1},{8,10},{10,12},{12... | collective-permute-start | bytes 196616 | tf_op jit(solution)/shard_map/ppermute | solution.py:216
  26.1 5.2 %collective-permute-start.1 = (bf16[256,128]{1,0:T(8,128)(2,1)S(1)}, bf16[256,128]{1,0:T(8,128)(2,1)S(1)}, u32[]{:S(2)}, u32[]{:S(2)}) collective-permute-start(bf16[256,128]{1,0:T(8,128)(2,1)S(1)} %bitcast.10), channel_id=1, source_target_pairs={{0,4},{2,6},{4,0},{6,2},{1,5},{3,7},{5,1},{7,3},{8,12},{10,14},{12... | collective-permute-start | bytes 196616 | tf_op jit(solution)/shard_map/ppermute | solution.py:216
  28.7 3.4 %collective-permute-start = (bf16[256,128]{1,0:T(8,128)(2,1)S(1)}, bf16[256,128]{1,0:T(8,128)(2,1)S(1)}, u32[]{:S(2)}, u32[]{:S(2)}) collective-permute-start(bf16[256,128]{1,0:T(8,128)(2,1)S(1)} %bitcast.11), channel_id=1, source_target_pairs={{0,6},{2,0},{4,2},{6,4},{1,7},{3,1},{5,3},{7,5},{8,14},{10,8},{12,... | collective-permute-start | bytes 196616 | tf_op jit(solution)/shard_map/ppermute | solution.py:216

commit v7 on v6

--- a/solution.py
+++ b/solution.py
@@ -63,6 +63,11 @@
     pltpu.make_async_copy(start_hbm, start_ref, sems.at[1]).start()
     for tile in range(SAMPLES // LANES):
         pltpu.make_async_copy(volt_hbm.at[:, :, pl.ds(tile * LANES, LANES)], volt_ref.at[tile], sems.at[2]).start()
+
+    @pl.when(first)
+    def _():
+        hist_copy.start()
+
     lane = lax.broadcasted_iota(jnp.int32, (2 * CHANNELS, LANES), 1)
     past_ref[...] = jnp.zeros((2 * CHANNELS, LANES), jnp.float32)
     pltpu.make_async_copy(window_hbm, window_ref, sems.at[0]).wait()
@@ -70,7 +75,6 @@
 
     @pl.when(first)
     def _():
-        hist_copy.start()
         hist_copy.wait()
 
         def frames_at(step):

time: 34 us -> 34 us (level)
  blocking collectives: 21.1 us -> 21.7 us
  Pallas kernels: 5.65 us -> 5.09 us
    pallas_call x1, Pallas kernels: 3.66 us -> 3.1 us  [body(): pl.pallas_call(transform_kernel, out_shape=pltpu.VMEM((2 * LANES, LANES),...]
    all_to_all x1, blocking collectives: 21.1 us -> 21.7 us  [body(): lax.all_to_all(chunks, ('x', 'zl', 'c', 'zh'), 0, 0, tiled=True)]
where the time goes in v7:
time: 34 us; the launch traced here: 33.7 us
  blocking collectives  21.7 us (64%)
  Pallas kernels  5.09 us (15%)
  starting transfers between devices  4.99 us (15%)
  waiting for transfers between devices  1.91 us (6%)
    all_to_all x1, blocking collectives, body(): lax.all_to_all(chunks, ('x', 'zl', 'c', 'zh'), 0, 0, tiled=True)  21.7 us
    ppermute x3, starting transfers between devices, body(): lax.ppermute(mine, 'y', [(i, (i + k) % 4) for i in range(4)])  4.99 us
    pallas_call x1, Pallas kernels, body(): pl.pallas_call(transform_kernel, out_shape=pltpu.VMEM((2 * LANES, LANES),...  3.1 us
    ppermute x3, waiting for transfers between devices, body(): lax.ppermute(mine, 'y', [(i, (i + k) % 4) for i in range(4)])  1.91 us
    pallas_call x1, Pallas kernels, body(): pl.pallas_call(gram_kernel, out_shape=jax.ShapeDtypeStruct((LANES, 8, 2,...  1.42 us
  transfers between devices with their start and end apart: 3, of which 2 were waited for; matrix products, arithmetic and copies ran while one was open for 0% of the time, Pallas kernels for 1%

profile of v7, /device:TPU:1, one launch (start us, length us, event | category | flops | bytes accessed | tf_op | source)
XLA Modules:
  0.0 33.7 jit_solution(14395403596959182002)
XLA Ops:
  0.0 3.1 %transform.1 = bf16[256,128]{1,0:T(8,128)(2,1)S(1)} custom-call(bf16[32,4,2048]{2,1,0:T(4,128)(2,1)} %volt_hbm.1, bf16[96,2048]{1,0:T(8,128)(2,1)} %bitcast.13, f32[4,2048]{1,0:T(4,128)} %window_hbm.1, f32[128,128]{1,0:T(8,128)} %constant.2.clone.start_hbm), custom_call_target="tpu_custom_call" | custom-call | tf_op jit(solution)/shard_map/transform/pallas_call | solution.py:202
  3.1 21.7 %all_to_all.5 = bf16[64,4,128]{2,1,0:T(4,128)(2,1)S(1)} all-to-all(bf16[64,4,128]{2,1,0:T(4,128)(2,1)S(1)} %bitcast.8), channel_id=1, replica_groups=mesh['x'=4,'zl'=4,'c'=2,'y'=4,'zh'=2] {'x','zl','c','zh'}, dimensions={0} | all-to-all | bytes 131072 | tf_op jit(solution)/shard_map/all_to_all | solution.py:219
  24.8 1.3 %collective-permute-start.2 = (bf16[256,128]{1,0:T(8,128)(2,1)S(1)}, bf16[256,128]{1,0:T(8,128)(2,1)S(1)}, u32[]{:S(2)}, u32[]{:S(2)}) collective-permute-start(bf16[256,128]{1,0:T(8,128)(2,1)S(1)} %bitcast.9), channel_id=1, source_target_pairs={{0,2},{2,4},{4,6},{6,0},{1,3},{3,5},{5,7},{7,1},{8,10},{10,12},{12... | collective-permute-start | bytes 196616 | tf_op jit(solution)/shard_map/ppermute | solution.py:220
  26.1 2.6 %collective-permute-start.1 = (bf16[256,128]{1,0:T(8,128)(2,1)S(1)}, bf16[256,128]{1,0:T(8,128)(2,1)S(1)}, u32[]{:S(2)}, u32[]{:S(2)}) collective-permute-start(bf16[256,128]{1,0:T(8,128)(2,1)S(1)} %bitcast.10), channel_id=1, source_target_pairs={{0,4},{2,6},{4,0},{6,2},{1,5},{3,7},{5,1},{7,3},{8,12},{10,14},{12... | collective-permute-start | bytes 196616 | tf_op jit(solution)/shard_map/ppermute | solution.py:220
  28.7 1.1 %collective-permute-start = (bf16[256,128]{1,0:T(8,128)(2,1)S(1)}, bf16[256,128]{1,0:T(8,128)(2,1)S(1)}, u32[]{:S(2)}, u32[]{:S(2)}) collective-permute-start(bf16[256,128]{1,0:T(8,128)(2,1)S(1)} %bitcast.11), channel_id=1, source_target_pairs={{0,6},{2,0},{4,2},{6,4},{1,7},{3,1},{5,3},{7,5},{8,14},{10,8},{12,... | collective-permute-start | bytes 196616 | tf_op jit(solution)/shard_map/ppermute | solution.py:220
  29.8 0.1 decode3.1
  29.9 0.0 collective-permute-done.2.got_ref
  29.9 0.1 decode2.1
  30.1 1.2 %collective-permute-done.1.got_ref = bf16[256,128]{1,0:T(8,128)(2,1)S(1)} collective-permute-done((bf16[256,128]{1,0:T(8,128)(2,1)S(1)}, bf16[256,128]{1,0:T(8,128)(2,1)S(1)}, u32[]{:S(2)}, u32[]{:S(2)}) %collective-permute-start.1) | collective-permute-done | bytes 65568 | tf_op jit(solution)/shard_map/ppermute | solution.py:220
  31.3 0.1 decode1.1
  31.5 0.7 %collective-permute-done.got_ref = bf16[256,128]{1,0:T(8,128)(2,1)S(1)} collective-permute-done((bf16[256,128]{1,0:T(8,128)(2,1)S(1)}, bf16[256,128]{1,0:T(8,128)(2,1)S(1)}, u32[]{:S(2)}, u32[]{:S(2)}) %collective-permute-start) | collective-permute-done | bytes 65568 | tf_op jit(solution)/shard_map/ppermute | solution.py:220
  32.1 0.1 decode0.1
  32.3 1.4 %gram.1 = f32[128,8,2,128]{3,2,1,0:T(2,128)} custom-call(f32[8,16,128]{2,1,0:T(8,128)S(1)} %get-tuple-element.13.refs_0_, f32[8,16,128]{2,1,0:T(8,128)S(1)} %get-tuple-element.14.refs_1_, f32[8,16,128]{2,1,0:T(8,128)S(1)} %get-tuple-element.15.refs_2_, f32[8,16,128]{2,1,0:T(8,128)S(1)} %get-tuple-element.16.refs_3_, ...), custom_call_target="tpu_custom_call" | custom-call | tf_op jit(solution)/shard_map/gram/pallas_call | solution.py:232
Async XLA Ops:
  24.8 5.1 %collective-permute-start.2 = (bf16[256,128]{1,0:T(8,128)(2,1)S(1)}, bf16[256,128]{1,0:T(8,128)(2,1)S(1)}, u32[]{:S(2)}, u32[]{:S(2)}) collective-permute-start(bf16[256,128]{1,0:T(8,128)(2,1)S(1)} %bitcast.9), channel_id=1, source_target_pairs={{0,2},{2,4},{4,6},{6,0},{1,3},{3,5},{5,7},{7,1},{8,10},{10,12},{12... | collective-permute-start | bytes 196616 | tf_op jit(solution)/shard_map/ppermute | solution.py:220
  26.1 5.2 %collective-permute-start.1 = (bf16[256,128]{1,0:T(8,128)(2,1)S(1)}, bf16[256,128]{1,0:T(8,128)(2,1)S(1)}, u32[]{:S(2)}, u32[]{:S(2)}) collective-permute-start(bf16[256,128]{1,0:T(8,128)(2,1)S(1)} %bitcast.10), channel_id=1, source_target_pairs={{0,4},{2,6},{4,0},{6,2},{1,5},{3,7},{5,1},{7,3},{8,12},{10,14},{12... | collective-permute-start | bytes 196616 | tf_op jit(solution)/shard_map/ppermute | solution.py:220
  28.7 3.4 %collective-permute-start = (bf16[256,128]{1,0:T(8,128)(2,1)S(1)}, bf16[256,128]{1,0:T(8,128)(2,1)S(1)}, u32[]{:S(2)}, u32[]{:S(2)}) collective-permute-start(bf16[256,128]{1,0:T(8,128)(2,1)S(1)} %bitcast.11), channel_id=1, source_target_pairs={{0,6},{2,0},{4,2},{6,4},{1,7},{3,1},{5,3},{7,5},{8,14},{10,8},{12,... | collective-permute-start | bytes 196616 | tf_op jit(solution)/shard_map/ppermute | solution.py:220

commit v8 on v7

--- a/solution.py
+++ b/solution.py
@@ -49,9 +49,9 @@
         weights = jnp.concatenate([table * window_ref[tap : tap + 1, cols] for tap in range(taps)], axis=0)
         high, low = two_terms(weights)
         frames = frames_at(step)
-        part = lax.dot_general(high, frames, dims, preferred_element_type=jnp.float32)
-        part = part + lax.dot_general(low, frames, dims, preferred_element_type=jnp.float32)
+        part = lax.dot_general(jnp.concatenate([high, low], axis=0), frames, dims, preferred_element_type=jnp.float32)
         total = part if total is None else total + part
+    total = total[: total.shape[0] // 2] + total[total.shape[0] // 2 :]
     return [total[tap * 2 * CHANNELS : (tap + 1) * 2 * CHANNELS] for tap in range(taps)]
 
 

time: 34 us -> 34 us (level)
  no operation moved by 1% of the time
where the time goes in v8:
time: 34 us; the launch traced here: 33.7 us
  blocking collectives  21.7 us (64%)
  Pallas kernels  5.05 us (15%)
  starting transfers between devices  4.99 us (15%)
  waiting for transfers between devices  1.91 us (6%)
    all_to_all x1, blocking collectives, body(): lax.all_to_all(chunks, ('x', 'zl', 'c', 'zh'), 0, 0, tiled=True)  21.7 us
    ppermute x3, starting transfers between devices, body(): lax.ppermute(mine, 'y', [(i, (i + k) % 4) for i in range(4)])  4.99 us
    pallas_call x1, Pallas kernels, body(): pl.pallas_call(transform_kernel, out_shape=pltpu.VMEM((2 * LANES, LANES),...  3.07 us
    ppermute x3, waiting for transfers between devices, body(): lax.ppermute(mine, 'y', [(i, (i + k) % 4) for i in range(4)])  1.91 us
    pallas_call x1, Pallas kernels, body(): pl.pallas_call(gram_kernel, out_shape=jax.ShapeDtypeStruct((LANES, 8, 2,...  1.42 us
  transfers between devices with their start and end apart: 3, of which 2 were waited for; matrix products, arithmetic and copies ran while one was open for 0% of the time, Pallas kernels for 1%

profile of v8, /device:TPU:1, one launch (start us, length us, event | category | flops | bytes accessed | tf_op | source)
XLA Modules:
  0.0 33.7 jit_solution(17744674690213301051)
XLA Ops:
  0.0 3.1 %transform.1 = bf16[256,128]{1,0:T(8,128)(2,1)S(1)} custom-call(bf16[32,4,2048]{2,1,0:T(4,128)(2,1)} %volt_hbm.1, bf16[96,2048]{1,0:T(8,128)(2,1)} %bitcast.13, f32[4,2048]{1,0:T(4,128)} %window_hbm.1, f32[128,128]{1,0:T(8,128)} %constant.2.clone.start_hbm), custom_call_target="tpu_custom_call" | custom-call | tf_op jit(solution)/shard_map/transform/pallas_call | solution.py:202
  3.1 21.7 %all_to_all.5 = bf16[64,4,128]{2,1,0:T(4,128)(2,1)S(1)} all-to-all(bf16[64,4,128]{2,1,0:T(4,128)(2,1)S(1)} %bitcast.8), channel_id=1, replica_groups=mesh['x'=4,'zl'=4,'c'=2,'y'=4,'zh'=2] {'x','zl','c','zh'}, dimensions={0} | all-to-all | bytes 131072 | tf_op jit(solution)/shard_map/all_to_all | solution.py:219
  24.8 1.3 %collective-permute-start.2 = (bf16[256,128]{1,0:T(8,128)(2,1)S(1)}, bf16[256,128]{1,0:T(8,128)(2,1)S(1)}, u32[]{:S(2)}, u32[]{:S(2)}) collective-permute-start(bf16[256,128]{1,0:T(8,128)(2,1)S(1)} %bitcast.9), channel_id=1, source_target_pairs={{0,2},{2,4},{4,6},{6,0},{1,3},{3,5},{5,7},{7,1},{8,10},{10,12},{12... | collective-permute-start | bytes 196616 | tf_op jit(solution)/shard_map/ppermute | solution.py:220
  26.1 2.6 %collective-permute-start.1 = (bf16[256,128]{1,0:T(8,128)(2,1)S(1)}, bf16[256,128]{1,0:T(8,128)(2,1)S(1)}, u32[]{:S(2)}, u32[]{:S(2)}) collective-permute-start(bf16[256,128]{1,0:T(8,128)(2,1)S(1)} %bitcast.10), channel_id=1, source_target_pairs={{0,4},{2,6},{4,0},{6,2},{1,5},{3,7},{5,1},{7,3},{8,12},{10,14},{12... | collective-permute-start | bytes 196616 | tf_op jit(solution)/shard_map/ppermute | solution.py:220
  28.7 1.1 %collective-permute-start = (bf16[256,128]{1,0:T(8,128)(2,1)S(1)}, bf16[256,128]{1,0:T(8,128)(2,1)S(1)}, u32[]{:S(2)}, u32[]{:S(2)}) collective-permute-start(bf16[256,128]{1,0:T(8,128)(2,1)S(1)} %bitcast.11), channel_id=1, source_target_pairs={{0,6},{2,0},{4,2},{6,4},{1,7},{3,1},{5,3},{7,5},{8,14},{10,8},{12,... | collective-permute-start | bytes 196616 | tf_op jit(solution)/shard_map/ppermute | solution.py:220
  29.8 0.1 decode3.1
  29.9 0.0 collective-permute-done.2.got_ref
  29.9 0.1 decode2.1
  30.1 1.2 %collective-permute-done.1.got_ref = bf16[256,128]{1,0:T(8,128)(2,1)S(1)} collective-permute-done((bf16[256,128]{1,0:T(8,128)(2,1)S(1)}, bf16[256,128]{1,0:T(8,128)(2,1)S(1)}, u32[]{:S(2)}, u32[]{:S(2)}) %collective-permute-start.1) | collective-permute-done | bytes 65568 | tf_op jit(solution)/shard_map/ppermute | solution.py:220
  31.3 0.1 decode1.1
  31.5 0.7 %collective-permute-done.got_ref = bf16[256,128]{1,0:T(8,128)(2,1)S(1)} collective-permute-done((bf16[256,128]{1,0:T(8,128)(2,1)S(1)}, bf16[256,128]{1,0:T(8,128)(2,1)S(1)}, u32[]{:S(2)}, u32[]{:S(2)}) %collective-permute-start) | collective-permute-done | bytes 65568 | tf_op jit(solution)/shard_map/ppermute | solution.py:220
  32.1 0.1 decode0.1
  32.3 1.4 %gram.1 = f32[128,8,2,128]{3,2,1,0:T(2,128)} custom-call(f32[8,16,128]{2,1,0:T(8,128)S(1)} %get-tuple-element.13.refs_0_, f32[8,16,128]{2,1,0:T(8,128)S(1)} %get-tuple-element.14.refs_1_, f32[8,16,128]{2,1,0:T(8,128)S(1)} %get-tuple-element.15.refs_2_, f32[8,16,128]{2,1,0:T(8,128)S(1)} %get-tuple-element.16.refs_3_, ...), custom_call_target="tpu_custom_call" | custom-call | tf_op jit(solution)/shard_map/gram/pallas_call | solution.py:232
Async XLA Ops:
  24.8 5.1 %collective-permute-start.2 = (bf16[256,128]{1,0:T(8,128)(2,1)S(1)}, bf16[256,128]{1,0:T(8,128)(2,1)S(1)}, u32[]{:S(2)}, u32[]{:S(2)}) collective-permute-start(bf16[256,128]{1,0:T(8,128)(2,1)S(1)} %bitcast.9), channel_id=1, source_target_pairs={{0,2},{2,4},{4,6},{6,0},{1,3},{3,5},{5,7},{7,1},{8,10},{10,12},{12... | collective-permute-start | bytes 196616 | tf_op jit(solution)/shard_map/ppermute | solution.py:220
  26.1 5.2 %collective-permute-start.1 = (bf16[256,128]{1,0:T(8,128)(2,1)S(1)}, bf16[256,128]{1,0:T(8,128)(2,1)S(1)}, u32[]{:S(2)}, u32[]{:S(2)}) collective-permute-start(bf16[256,128]{1,0:T(8,128)(2,1)S(1)} %bitcast.10), channel_id=1, source_target_pairs={{0,4},{2,6},{4,0},{6,2},{1,5},{3,7},{5,1},{7,3},{8,12},{10,14},{12... | collective-permute-start | bytes 196616 | tf_op jit(solution)/shard_map/ppermute | solution.py:220
  28.7 3.4 %collective-permute-start = (bf16[256,128]{1,0:T(8,128)(2,1)S(1)}, bf16[256,128]{1,0:T(8,128)(2,1)S(1)}, u32[]{:S(2)}, u32[]{:S(2)}) collective-permute-start(bf16[256,128]{1,0:T(8,128)(2,1)S(1)} %bitcast.11), channel_id=1, source_target_pairs={{0,6},{2,0},{4,2},{6,4},{1,7},{3,1},{5,3},{7,5},{8,14},{10,8},{12,... | collective-permute-start | bytes 196616 | tf_op jit(solution)/shard_map/ppermute | solution.py:220

commit v9 on v8

--- a/solution.py
+++ b/solution.py
@@ -138,7 +138,7 @@
     out_ref[...] = rows_ref[...].astype(jnp.bfloat16)
 
 
-def decode_kernel(got_ref, sums_ref, passed_ref):
+def decode_kernel(got_ref, sums_ref, passed_ref, *order_ref):
     lane_group = lax.broadcasted_iota(jnp.int32, (8, LANES), 1) // IN_BLK
     row = lax.broadcasted_iota(jnp.int32, (8, LANES), 0)
     upper = row % 4 >= 2
@@ -162,10 +162,15 @@
         second = jnp.where(row < 4, pltpu.roll(moved[1], 2, 0), 0.0)
         passed_ref[tile, :8, :] = jnp.where(row < 2, moved[0], second)
         passed_ref[tile, 8:, :] = jnp.where(row < 2, moved[2], 0.0)
+    if order_ref:
+        row = lax.broadcasted_iota(jnp.int32, (2 * LANES, 2 * LANES), 0)
+        col = lax.broadcasted_iota(jnp.int32, (2 * LANES, 2 * LANES), 1)
+        order = jnp.where(col == row % 2 * LANES + row // 2, 1.0, 0.0)
+        order_ref[0][...] = order.astype(jnp.bfloat16)
 
 
 def gram_kernel(*refs):
-    sums_refs, passed_refs, out_hbm, vis_ref, sems = refs[:4], refs[4:8], *refs[8:]
+    sums_refs, passed_refs, order_ref, out_hbm, vis_ref, sems = refs[:4], refs[4:8], *refs[8:]
 
     def frames_of(tile):
         return jnp.concatenate([sums_refs[i][tile] + passed_refs[i - 1][tile] for i in range(4)], axis=0)
@@ -176,10 +181,7 @@
     turned = jnp.where(real, pltpu.roll(left, left.shape[0] - 1, 0), -pltpu.roll(left, 1, 0))
     high, low = two_terms(jnp.concatenate([left, turned], axis=1))
     left = jnp.concatenate([high, high, low], axis=0)
-    row = lax.broadcasted_iota(jnp.int32, (2 * LANES, 2 * LANES), 0)
-    col = lax.broadcasted_iota(jnp.int32, (2 * LANES, 2 * LANES), 1)
-    order = jnp.where(col == row % 2 * LANES + row // 2, 1.0, 0.0).astype(jnp.bfloat16)
-    left = lax.dot_general(order, left, (((1,), (1,)), ((), ())), preferred_element_type=jnp.float32)
+    left = lax.dot_general(order_ref[...], left, (((1,), (1,)), ((), ())), preferred_element_type=jnp.float32)
     left = left.astype(jnp.bfloat16)
     copies = []
     for pair in range(4):
@@ -220,11 +222,12 @@
     ahead, behind, across = (lax.ppermute(mine, "y", [(i, (i + k) % 4) for i in range(4)]) for k in (1, 3, 2))
     sums, passed = [], []
     for i, piece in enumerate((behind, across, ahead, mine)):
+        extra = [pltpu.VMEM((2 * LANES, 2 * LANES), jnp.bfloat16)] if i == 3 else []
         found = pl.pallas_call(
             decode_kernel,
-            out_shape=[pltpu.VMEM((8, 2 * 8, LANES), jnp.float32)] * 2,
+            out_shape=[pltpu.VMEM((8, 2 * 8, LANES), jnp.float32)] * 2 + extra,
             in_specs=[vmem],
-            out_specs=[vmem] * 2,
+            out_specs=[vmem] * (2 + len(extra)),
             name=f"decode{i}",
         )(pltpu.with_memory_space_constraint(piece, pltpu.VMEM))
         sums.append(pltpu.with_memory_space_constraint(found[0], pltpu.VMEM))
@@ -232,11 +235,11 @@
     tiles = pl.pallas_call(
         gram_kernel,
         out_shape=jax.ShapeDtypeStruct((LANES, 8, 2, LANES), jnp.float32),
-        in_specs=[vmem] * 8,
+        in_specs=[vmem] * 9,
         out_specs=hbm,
         scratch_shapes=[pltpu.VMEM((8, LANES, 2, LANES), jnp.float32), pltpu.SemaphoreType.DMA((8,))],
         name="gram",
-    )(*sums, *passed)
+    )(*sums, *passed, pltpu.with_memory_space_constraint(found[2], pltpu.VMEM))
     return tiles.transpose(0, 2, 1, 3).reshape(LANES, 1, 2, 8 * LANES)
 
 

time: 34 us -> 34 us (level)
  no operation moved by 1% of the time
where the time goes in v9:
time: 34 us; the launch traced here: 33.7 us
  blocking collectives  21.7 us (64%)
  Pallas kernels  5.05 us (15%)
  starting transfers between devices  4.99 us (15%)
  waiting for transfers between devices  1.9 us (6%)
    all_to_all x1, blocking collectives, body(): lax.all_to_all(chunks, ('x', 'zl', 'c', 'zh'), 0, 0, tiled=True)  21.7 us
    ppermute x3, starting transfers between devices, body(): lax.ppermute(mine, 'y', [(i, (i + k) % 4) for i in range(4)])  4.99 us
    pallas_call x1, Pallas kernels, body(): pl.pallas_call(transform_kernel, out_shape=pltpu.VMEM((2 * LANES, LANES),...  3.07 us
    ppermute x3, waiting for transfers between devices, body(): lax.ppermute(mine, 'y', [(i, (i + k) % 4) for i in range(4)])  1.9 us
    pallas_call x1, Pallas kernels, body(): pl.pallas_call(gram_kernel, out_shape=jax.ShapeDtypeStruct((LANES, 8, 2,...  1.42 us
  transfers between devices with their start and end apart: 3, of which 2 were waited for; matrix products, arithmetic and copies ran while one was open for 0% of the time, Pallas kernels for 1%

profile of v9, /device:TPU:1, one launch (start us, length us, event | category | flops | bytes accessed | tf_op | source)
XLA Modules:
  0.0 33.7 jit_solution(15532347502412248044)
XLA Ops:
  0.0 3.1 %transform.1 = bf16[256,128]{1,0:T(8,128)(2,1)S(1)} custom-call(bf16[32,4,2048]{2,1,0:T(4,128)(2,1)} %volt_hbm.1, bf16[96,2048]{1,0:T(8,128)(2,1)} %bitcast.13, f32[4,2048]{1,0:T(4,128)} %window_hbm.1, f32[128,128]{1,0:T(8,128)} %constant.2.clone.start_hbm), custom_call_target="tpu_custom_call" | custom-call | tf_op jit(solution)/shard_map/transform/pallas_call | solution.py:204
  3.1 21.7 %all_to_all.5 = bf16[64,4,128]{2,1,0:T(4,128)(2,1)S(1)} all-to-all(bf16[64,4,128]{2,1,0:T(4,128)(2,1)S(1)} %bitcast.8), channel_id=1, replica_groups=mesh['x'=4,'zl'=4,'c'=2,'y'=4,'zh'=2] {'x','zl','c','zh'}, dimensions={0} | all-to-all | bytes 131072 | tf_op jit(solution)/shard_map/all_to_all | solution.py:221
  24.8 1.3 %collective-permute-start.2 = (bf16[256,128]{1,0:T(8,128)(2,1)S(1)}, bf16[256,128]{1,0:T(8,128)(2,1)S(1)}, u32[]{:S(2)}, u32[]{:S(2)}) collective-permute-start(bf16[256,128]{1,0:T(8,128)(2,1)S(1)} %bitcast.9), channel_id=1, source_target_pairs={{0,2},{2,4},{4,6},{6,0},{1,3},{3,5},{5,7},{7,1},{8,10},{10,12},{12... | collective-permute-start | bytes 196616 | tf_op jit(solution)/shard_map/ppermute | solution.py:222
  26.1 2.6 %collective-permute-start.1 = (bf16[256,128]{1,0:T(8,128)(2,1)S(1)}, bf16[256,128]{1,0:T(8,128)(2,1)S(1)}, u32[]{:S(2)}, u32[]{:S(2)}) collective-permute-start(bf16[256,128]{1,0:T(8,128)(2,1)S(1)} %bitcast.10), channel_id=1, source_target_pairs={{0,4},{2,6},{4,0},{6,2},{1,5},{3,7},{5,1},{7,3},{8,12},{10,14},{12... | collective-permute-start | bytes 196616 | tf_op jit(solution)/shard_map/ppermute | solution.py:222
  28.7 1.1 %collective-permute-start = (bf16[256,128]{1,0:T(8,128)(2,1)S(1)}, bf16[256,128]{1,0:T(8,128)(2,1)S(1)}, u32[]{:S(2)}, u32[]{:S(2)}) collective-permute-start(bf16[256,128]{1,0:T(8,128)(2,1)S(1)} %bitcast.11), channel_id=1, source_target_pairs={{0,6},{2,0},{4,2},{6,4},{1,7},{3,1},{5,3},{7,5},{8,14},{10,8},{12,... | collective-permute-start | bytes 196616 | tf_op jit(solution)/shard_map/ppermute | solution.py:222
  29.8 0.1 decode3.1
  29.9 0.0 collective-permute-done.2.got_ref
  29.9 0.1 decode2.1
  30.1 1.2 %collective-permute-done.1.got_ref = bf16[256,128]{1,0:T(8,128)(2,1)S(1)} collective-permute-done((bf16[256,128]{1,0:T(8,128)(2,1)S(1)}, bf16[256,128]{1,0:T(8,128)(2,1)S(1)}, u32[]{:S(2)}, u32[]{:S(2)}) %collective-permute-start.1) | collective-permute-done | bytes 65568 | tf_op jit(solution)/shard_map/ppermute | solution.py:222
  31.3 0.1 decode1.1
  31.5 0.7 %collective-permute-done.got_ref = bf16[256,128]{1,0:T(8,128)(2,1)S(1)} collective-permute-done((bf16[256,128]{1,0:T(8,128)(2,1)S(1)}, bf16[256,128]{1,0:T(8,128)(2,1)S(1)}, u32[]{:S(2)}, u32[]{:S(2)}) %collective-permute-start) | collective-permute-done | bytes 65568 | tf_op jit(solution)/shard_map/ppermute | solution.py:222
  32.1 0.1 decode0.1
  32.3 1.4 %gram.1 = f32[128,8,2,128]{3,2,1,0:T(2,128)} custom-call(f32[8,16,128]{2,1,0:T(8,128)S(1)} %get-tuple-element.14.refs_0_, f32[8,16,128]{2,1,0:T(8,128)S(1)} %get-tuple-element.15.refs_1_, f32[8,16,128]{2,1,0:T(8,128)S(1)} %get-tuple-element.16.refs_2_, f32[8,16,128]{2,1,0:T(8,128)S(1)} %get-tuple-element.17.refs_3_, ...), custom_call_target="tpu_custom_call" | custom-call | tf_op jit(solution)/shard_map/gram/pallas_call | solution.py:235
Async XLA Ops:
  24.8 5.1 %collective-permute-start.2 = (bf16[256,128]{1,0:T(8,128)(2,1)S(1)}, bf16[256,128]{1,0:T(8,128)(2,1)S(1)}, u32[]{:S(2)}, u32[]{:S(2)}) collective-permute-start(bf16[256,128]{1,0:T(8,128)(2,1)S(1)} %bitcast.9), channel_id=1, source_target_pairs={{0,2},{2,4},{4,6},{6,0},{1,3},{3,5},{5,7},{7,1},{8,10},{10,12},{12... | collective-permute-start | bytes 196616 | tf_op jit(solution)/shard_map/ppermute | solution.py:222
  26.1 5.2 %collective-permute-start.1 = (bf16[256,128]{1,0:T(8,128)(2,1)S(1)}, bf16[256,128]{1,0:T(8,128)(2,1)S(1)}, u32[]{:S(2)}, u32[]{:S(2)}) collective-permute-start(bf16[256,128]{1,0:T(8,128)(2,1)S(1)} %bitcast.10), channel_id=1, source_target_pairs={{0,4},{2,6},{4,0},{6,2},{1,5},{3,7},{5,1},{7,3},{8,12},{10,14},{12... | collective-permute-start | bytes 196616 | tf_op jit(solution)/shard_map/ppermute | solution.py:222
  28.7 3.4 %collective-permute-start = (bf16[256,128]{1,0:T(8,128)(2,1)S(1)}, bf16[256,128]{1,0:T(8,128)(2,1)S(1)}, u32[]{:S(2)}, u32[]{:S(2)}) collective-permute-start(bf16[256,128]{1,0:T(8,128)(2,1)S(1)} %bitcast.11), channel_id=1, source_target_pairs={{0,6},{2,0},{4,2},{6,4},{1,7},{3,1},{5,3},{7,5},{8,14},{10,8},{12,... | collective-permute-start | bytes 196616 | tf_op jit(solution)/shard_map/ppermute | solution.py:222
